TPU v7x, 512 devices: a whole 4x4x16 slice. The times are simulated.
512 devices in a mesh: gx: 16 (over z), gz: 32 (over x, y, core).
Axes of the slice: x: 4, y: 4, z: 16, core: 2. Of those that a mesh axis runs over, the one named last changes fastest.
Arguments:
- velocity: float32 [3, 4096, 1, 4096], P(None, 'gx', None, 'gz'), may hold values from -6 to 6
Outputs:
- advection: float32 [3, 4096, 1, 4096], P(None, 'gx', None, 'gz')
All inputs are finite; a program needn't handle non-finite values.
Results may differ from a plain program's by a relative error of at most 0.00013.
Values sent between devices are 32-bit elements; how exact they have to be, the bound alone decides.
A program may use at most 64 MiB of HBM per device.

v0:
```python
import jax
import jax.numpy as jnp
from jax import lax
from jax.sharding import PartitionSpec as P

ALPHA_D = 1.0 / 3.0
COEF_A = 14.0 / 9.0
COEF_B = 1.0 / 9.0
ALPHA_F = 0.49
block_len = 128


def with_halo(block, sides, width):
    for axis, dim in sides:
        count = lax.axis_size(axis)
        forward = [(i, i + 1) for i in range(count - 1)]
        forward.append((count - 1, 0))
        backward = [(target, source) for source, target in forward]
        low = lax.ppermute(
            lax.slice_in_dim(block, block.shape[dim] - width, None, axis=dim), axis, forward
        )
        high = lax.ppermute(lax.slice_in_dim(block, 0, width, axis=dim), axis, backward)
        block = jnp.concatenate([low, block, high], axis=dim)
    return block


def filter_coefficients():
    return (
        (11.0 + 10.0 * ALPHA_F) / 16.0,
        (15.0 + 34.0 * ALPHA_F) / 32.0,
        (-3.0 + 6.0 * ALPHA_F) / 16.0,
        (1.0 - 2.0 * ALPHA_F) / 32.0,
    )


def tables(length, alpha):
    lower_diag = jnp.concatenate(
        [jnp.zeros((1,), jnp.float32), jnp.full((length - 1,), alpha, jnp.float32)]
    )
    upper_diag = jnp.concatenate(
        [jnp.full((length - 1,), alpha, jnp.float32), jnp.zeros((1,), jnp.float32)]
    )
    main_diag = jnp.ones((length,), jnp.float32)
    identity = jnp.eye(length, dtype=jnp.float32)
    inverse = lax.linalg.tridiagonal_solve(lower_diag, main_diag, upper_diag, identity)
    left_col = alpha * inverse[:, 0]
    right_col = alpha * inverse[:, length - 1]
    coupling = alpha * inverse[0, 0]
    return (inverse, left_col, right_col, coupling)


def offset_slice(extended, offset, length, direction, base=3):
    return lax.slice_in_dim(extended, base + offset, base + offset + length, axis=direction)


def slope_rhs(extended, length, direction, base=3):
    rhs = (
        COEF_A
        * 0.5
        * (
            offset_slice(extended, 1, length, direction, base)
            - offset_slice(extended, -1, length, direction, base)
        )
    )
    return rhs + COEF_B * 0.25 * (
        offset_slice(extended, 2, length, direction, base)
        - offset_slice(extended, -2, length, direction, base)
    )


def smooth_rhs(extended, length, direction, base=3):
    coefficients = filter_coefficients()
    rhs = coefficients[0] * offset_slice(extended, 0, length, direction, base)
    for offset in range(1, 4):
        rhs = rhs + 0.5 * coefficients[offset] * (
            offset_slice(extended, offset, length, direction, base)
            + offset_slice(extended, -offset, length, direction, base)
        )
    return rhs


def wrap_pad(values, direction):
    length = values.shape[direction]
    return jnp.concatenate(
        [
            lax.slice_in_dim(values, length - 3, length, axis=direction),
            values,
            lax.slice_in_dim(values, 0, 3, axis=direction),
        ],
        axis=direction,
    )


def apply_along(inverse, values, direction):
    rotated = jnp.tensordot(
        inverse, values, axes=([1], [direction]), precision=lax.Precision.HIGHEST
    )
    return jnp.moveaxis(rotated, 0, direction)


def end_values(partial_value, direction):
    length = partial_value.shape[direction]
    first_val = lax.slice_in_dim(partial_value, 0, 1, axis=direction)
    last_val = lax.slice_in_dim(partial_value, length - 1, length, axis=direction)
    return (first_val, last_val)


def corrected(partial_value, prev_last, next_first, table, direction):
    inverse, left_col, right_col, coupling = table
    first_val, last_val = end_values(partial_value, direction)
    factor_inv = 1.0 / (1.0 - coupling * coupling)
    left_value = (prev_last - coupling * first_val) * factor_inv
    right_value = (next_first - coupling * last_val) * factor_inv
    dims_list = [1] * partial_value.ndim
    dims_list[direction] = partial_value.shape[direction]
    return (
        partial_value
        - left_col.reshape(dims_list) * left_value
        - right_col.reshape(dims_list) * right_value
    )


def extend_x(values):
    return with_halo(values, (("gx", 1),), 3)


def solve_x(rhs, table):
    partial_value = apply_along(table[0], rhs, 1)
    first_val, last_val = end_values(partial_value, 1)
    beside = with_halo(jnp.concatenate([first_val, last_val], axis=1), (("gx", 1),), 1)
    return corrected(partial_value, beside[:, 0:1], beside[:, 3:4], table, 1)


def solve_blocks(rhs, table):
    dims_list = rhs.shape
    blocks = rhs.reshape(dims_list[:-1] + (dims_list[-1] // block_len, block_len))
    last_dim = blocks.ndim - 1
    partial_value = apply_along(table[0], blocks, last_dim)
    first_val, last_val = end_values(partial_value, last_dim)
    prev_last = jnp.roll(last_val, 1, axis=last_dim - 1)
    next_first = jnp.roll(first_val, -1, axis=last_dim - 1)
    return corrected(partial_value, prev_last, next_first, table, last_dim).reshape(dims_list)


def z_part(velocity):
    slope_z = tables(block_len, ALPHA_D)
    pencil = lax.all_to_all(velocity, "gz", split_axis=1, concat_axis=3, tiled=True)
    along_z = pencil[2:3]
    fields = jnp.concatenate([pencil, along_z * pencil], axis=0)
    slopes = solve_blocks(slope_rhs(wrap_pad(fields, 3), fields.shape[3], 3), slope_z)
    local_terms = slopes[3:] + along_z * slopes[:3]
    return lax.all_to_all(local_terms, "gz", split_axis=3, concat_axis=1, tiled=True)


def per_device(velocity):
    width_x = velocity.shape[1]
    slope_x = tables(width_x, ALPHA_D)
    smooth_x = tables(width_x, ALPHA_F)
    along_x = velocity[0:1]
    rim_source = jnp.concatenate([velocity, along_x * velocity], axis=0)
    padded = extend_x(rim_source)
    slopes_x = solve_x(slope_rhs(padded, width_x, 1), slope_x)
    x_terms = slopes_x[3:] + along_x * slopes_x[:3]
    z_terms = z_part(velocity)
    combined = 0.5 * (x_terms + z_terms)
    smoothed = solve_x(smooth_rhs(extend_x(combined), width_x, 1), smooth_x)
    return -smoothed


def solution(mesh):
    return jax.shard_map(
        per_device,
        mesh=mesh,
        in_specs=(P(None, "gx", None, "gz"),),
        out_specs=P(None, "gx", None, "gz"),
        check_vma=False,
    )
```

profile of v0, /device:TPU:1, one launch (start us, length us, event | category | flops | bytes accessed | tf_op | source)
XLA Modules:
  0.0 652.8 jit_solution(18233440407456017549)
XLA Ops:
  34.5 14.9 %while.98 = (s32[]{:T(128)}, f32[]{:T(128)}, f32[256]{0:T(256)S(1)}, f32[7,32]{1,0:T(8,128)S(1)}, f32[7,32,256]{2,1,0:T(8,128)S(1)}, /*index=5*/f32[7,32,256]{2,...) while((s32[]{:T(128)}, f32[]{:T(128)}, ...), condition=%wide.region_5.6_spmd, body=%wide.region_4.5_spmd.sunk | while | flops 24705 | bytes 267885 | solution.py:45
  69.1 64.5 %while.101 = (s32[]{:T(128)}, f32[128]{0:T(128)S(1)}, f32[3,32,128]{2,1,0:T(8,128)S(1)}, f32[3,32,128]{2,1,0:T(8,128)S(1)}, f32[3,32]{1,0:T(4,128)S(1)}, /*index...) while((s32[]{:T(128)}, f32[128]{0:T(128)S(1)}, ...), condition=%wide.region_11.12_spmd, body=%wide.region_10.11_spmd.sunk | while | flops 8226 | bytes 101341 | solution.py:45
  70.6 19.9 %fusion.491 = (f32[128]{0:T(128)S(1)}, f32[128]{0:T(128)S(1)}, f32[128]{0:T(128)S(1)}, f32[128]{0:T(128)S(1)}, f32[128]{0:T(128)S(1)}, /*index=5*/f32[128]{0:T(1...) fusion(f32[3,32,128]{2,1,0:T(8,128)S(1)} %get-tuple-element.256, ...), kind=kLoop, calls=%fused_computation.428.clone.1 | loop fusion | flops 8192 | bytes 33536 | tf_op jit(solution)/shard_map/while/body/eval_jaxpr/sub | solution.py:45
  92.1 19.9 %fusion.491 = (f32[128]{0:T(128)S(1)}, f32[128]{0:T(128)S(1)}, f32[128]{0:T(128)S(1)}, f32[128]{0:T(128)S(1)}, f32[128]{0:T(128)S(1)}, /*index=5*/f32[128]{0:T(1...) fusion(f32[3,32,128]{2,1,0:T(8,128)S(1)} %get-tuple-element.256, ...), kind=kLoop, calls=%fused_computation.428.clone.1 | loop fusion | flops 8192 | bytes 33536 | tf_op jit(solution)/shard_map/while/body/eval_jaxpr/sub | solution.py:45
  113.6 19.9 %fusion.491 = (f32[128]{0:T(128)S(1)}, f32[128]{0:T(128)S(1)}, f32[128]{0:T(128)S(1)}, f32[128]{0:T(128)S(1)}, f32[128]{0:T(128)S(1)}, /*index=5*/f32[128]{0:T(1...) fusion(f32[3,32,128]{2,1,0:T(8,128)S(1)} %get-tuple-element.256, ...), kind=kLoop, calls=%fused_computation.428.clone.1 | loop fusion | flops 8192 | bytes 33536 | tf_op jit(solution)/shard_map/while/body/eval_jaxpr/sub | solution.py:45
  176.4 153.7 %while.99 = (s32[]{:T(128)}, f32[256]{0:T(256)S(1)}, f32[7,32,256]{2,1,0:T(8,128)S(1)}, f32[7,32,256]{2,1,0:T(8,128)S(1)}, f32[7,32]{1,0:T(8,128)S(1)}, /*index=...) while((s32[]{:T(128)}, f32[256]{0:T(256)S(1)}, ...), condition=%wide.region_7.8_spmd, body=%wide.region_6.7_spmd.sunk | while | flops 16418 | bytes 266721 | solution.py:45
  178.1 20.2 %multiply_subtract_fusion.253 = (f32[256]{0:T(256)S(1)}, f32[256]{0:T(256)S(1)}, f32[256]{0:T(256)S(1)}, f32[256]{0:T(256)S(1)}, f32[256]{0:T(256)S(1)}, /*index...) fusion(f32[256]{0:T(256)S(1)} %bitcast.3158, ...), kind=kLoop, calls=%fused_computation.230.clone.1 | loop fusion | flops 16384 | bytes 66688 | tf_op jit(solution)/shard_map/while/body/eval_jaxpr/sub | solution.py:45
  200.0 20.2 %multiply_subtract_fusion.253 = (f32[256]{0:T(256)S(1)}, f32[256]{0:T(256)S(1)}, f32[256]{0:T(256)S(1)}, f32[256]{0:T(256)S(1)}, f32[256]{0:T(256)S(1)}, /*index...) fusion(f32[256]{0:T(256)S(1)} %bitcast.3158, ...), kind=kLoop, calls=%fused_computation.230.clone.1 | loop fusion | flops 16384 | bytes 66688 | tf_op jit(solution)/shard_map/while/body/eval_jaxpr/sub | solution.py:45
  222.0 20.2 %multiply_subtract_fusion.253 = (f32[256]{0:T(256)S(1)}, f32[256]{0:T(256)S(1)}, f32[256]{0:T(256)S(1)}, f32[256]{0:T(256)S(1)}, f32[256]{0:T(256)S(1)}, /*index...) fusion(f32[256]{0:T(256)S(1)} %bitcast.3158, ...), kind=kLoop, calls=%fused_computation.230.clone.1 | loop fusion | flops 16384 | bytes 66688 | tf_op jit(solution)/shard_map/while/body/eval_jaxpr/sub | solution.py:45
  244.0 20.2 %multiply_subtract_fusion.253 = (f32[256]{0:T(256)S(1)}, f32[256]{0:T(256)S(1)}, f32[256]{0:T(256)S(1)}, f32[256]{0:T(256)S(1)}, f32[256]{0:T(256)S(1)}, /*index...) fusion(f32[256]{0:T(256)S(1)} %bitcast.3158, ...), kind=kLoop, calls=%fused_computation.230.clone.1 | loop fusion | flops 16384 | bytes 66688 | tf_op jit(solution)/shard_map/while/body/eval_jaxpr/sub | solution.py:45
  265.9 20.2 %multiply_subtract_fusion.253 = (f32[256]{0:T(256)S(1)}, f32[256]{0:T(256)S(1)}, f32[256]{0:T(256)S(1)}, f32[256]{0:T(256)S(1)}, f32[256]{0:T(256)S(1)}, /*index...) fusion(f32[256]{0:T(256)S(1)} %bitcast.3158, ...), kind=kLoop, calls=%fused_computation.230.clone.1 | loop fusion | flops 16384 | bytes 66688 | tf_op jit(solution)/shard_map/while/body/eval_jaxpr/sub | solution.py:45
  287.9 20.2 %multiply_subtract_fusion.253 = (f32[256]{0:T(256)S(1)}, f32[256]{0:T(256)S(1)}, f32[256]{0:T(256)S(1)}, f32[256]{0:T(256)S(1)}, f32[256]{0:T(256)S(1)}, /*index...) fusion(f32[256]{0:T(256)S(1)} %bitcast.3158, ...), kind=kLoop, calls=%fused_computation.230.clone.1 | loop fusion | flops 16384 | bytes 66688 | tf_op jit(solution)/shard_map/while/body/eval_jaxpr/sub | solution.py:45
  309.8 20.2 %multiply_subtract_fusion.253 = (f32[256]{0:T(256)S(1)}, f32[256]{0:T(256)S(1)}, f32[256]{0:T(256)S(1)}, f32[256]{0:T(256)S(1)}, f32[256]{0:T(256)S(1)}, /*index...) fusion(f32[256]{0:T(256)S(1)} %bitcast.3158, ...), kind=kLoop, calls=%fused_computation.230.clone.1 | loop fusion | flops 16384 | bytes 66688 | tf_op jit(solution)/shard_map/while/body/eval_jaxpr/sub | solution.py:45
  330.1 19.3 %multiply_subtract_fusion.66 = (f32[256]{0:T(256)S(1)}, f32[256]{0:T(256)S(1)}, f32[256]{0:T(256)S(1)}, f32[256]{0:T(256)S(1)}, f32[256]{0:T(256)S(1)}, /*index=...) fusion(f32[256]{0:T(256)S(1)} %bitcast.3585, ...), kind=kLoop, calls=%fused_computation.598 | loop fusion | flops 15872 | bytes 64636 | tf_op jit(solution)/shard_map/eval_jaxpr/sub | solution.py:45
  351.8 152.3 %while.97 = (s32[]{:T(128)}, f32[256]{0:T(256)S(1)}, f32[7,32,256]{2,1,0:T(8,128)S(1)}, f32[7,32,256]{2,1,0:T(8,128)S(1)}, f32[7,32]{1,0:T(8,128)S(1)}, /*index=...) while((s32[]{:T(128)}, f32[256]{0:T(256)S(1)}, ...), condition=%wide.region_3.4_spmd, body=%wide.region_2.3_spmd.sunk | while | flops 16418 | bytes 266721 | solution.py:45
  353.4 20.0 %multiply_subtract_fusion.252 = (f32[256]{0:T(256)S(1)}, f32[256]{0:T(256)S(1)}, f32[256]{0:T(256)S(1)}, f32[256]{0:T(256)S(1)}, f32[256]{0:T(256)S(1)}, /*index...) fusion(f32[256]{0:T(256)S(1)} %bitcast.3176, ...), kind=kLoop, calls=%fused_computation.99.clone.1 | loop fusion | flops 16384 | bytes 66688 | tf_op jit(solution)/shard_map/while/body/eval_jaxpr/sub | solution.py:45
  375.2 20.0 %multiply_subtract_fusion.252 = (f32[256]{0:T(256)S(1)}, f32[256]{0:T(256)S(1)}, f32[256]{0:T(256)S(1)}, f32[256]{0:T(256)S(1)}, f32[256]{0:T(256)S(1)}, /*index...) fusion(f32[256]{0:T(256)S(1)} %bitcast.3176, ...), kind=kLoop, calls=%fused_computation.99.clone.1 | loop fusion | flops 16384 | bytes 66688 | tf_op jit(solution)/shard_map/while/body/eval_jaxpr/sub | solution.py:45
  396.9 20.0 %multiply_subtract_fusion.252 = (f32[256]{0:T(256)S(1)}, f32[256]{0:T(256)S(1)}, f32[256]{0:T(256)S(1)}, f32[256]{0:T(256)S(1)}, f32[256]{0:T(256)S(1)}, /*index...) fusion(f32[256]{0:T(256)S(1)} %bitcast.3176, ...), kind=kLoop, calls=%fused_computation.99.clone.1 | loop fusion | flops 16384 | bytes 66688 | tf_op jit(solution)/shard_map/while/body/eval_jaxpr/sub | solution.py:45
  418.7 20.0 %multiply_subtract_fusion.252 = (f32[256]{0:T(256)S(1)}, f32[256]{0:T(256)S(1)}, f32[256]{0:T(256)S(1)}, f32[256]{0:T(256)S(1)}, f32[256]{0:T(256)S(1)}, /*index...) fusion(f32[256]{0:T(256)S(1)} %bitcast.3176, ...), kind=kLoop, calls=%fused_computation.99.clone.1 | loop fusion | flops 16384 | bytes 66688 | tf_op jit(solution)/shard_map/while/body/eval_jaxpr/sub | solution.py:45
  440.4 20.0 %multiply_subtract_fusion.252 = (f32[256]{0:T(256)S(1)}, f32[256]{0:T(256)S(1)}, f32[256]{0:T(256)S(1)}, f32[256]{0:T(256)S(1)}, f32[256]{0:T(256)S(1)}, /*index...) fusion(f32[256]{0:T(256)S(1)} %bitcast.3176, ...), kind=kLoop, calls=%fused_computation.99.clone.1 | loop fusion | flops 16384 | bytes 66688 | tf_op jit(solution)/shard_map/while/body/eval_jaxpr/sub | solution.py:45
  462.2 20.0 %multiply_subtract_fusion.252 = (f32[256]{0:T(256)S(1)}, f32[256]{0:T(256)S(1)}, f32[256]{0:T(256)S(1)}, f32[256]{0:T(256)S(1)}, f32[256]{0:T(256)S(1)}, /*index...) fusion(f32[256]{0:T(256)S(1)} %bitcast.3176, ...), kind=kLoop, calls=%fused_computation.99.clone.1 | loop fusion | flops 16384 | bytes 66688 | tf_op jit(solution)/shard_map/while/body/eval_jaxpr/sub | solution.py:45
  483.9 20.0 %multiply_subtract_fusion.252 = (f32[256]{0:T(256)S(1)}, f32[256]{0:T(256)S(1)}, f32[256]{0:T(256)S(1)}, f32[256]{0:T(256)S(1)}, f32[256]{0:T(256)S(1)}, /*index...) fusion(f32[256]{0:T(256)S(1)} %bitcast.3176, ...), kind=kLoop, calls=%fused_computation.99.clone.1 | loop fusion | flops 16384 | bytes 66688 | tf_op jit(solution)/shard_map/while/body/eval_jaxpr/sub | solution.py:45
  536.5 22.9 %reduce.12 = f32[4096,3,8]{2,1,0:T(4,128)} reduce(f32[4096,3,1,8]{3,2,1,0:T(1,128)} %bitcast.2960, f32[]{:T(128)} %broadcast.790), dimensions={2}, to_apply=%bitcast.1784.reduce_sub_computation | reduce | bytes 786436
  621.6 19.3 %multiply_subtract_fusion.97 = (f32[256]{0:T(256)S(1)}, f32[256]{0:T(256)S(1)}, f32[256]{0:T(256)S(1)}, f32[256]{0:T(256)S(1)}, f32[256]{0:T(256)S(1)}, /*index=...) fusion(f32[256]{0:T(256)S(1)} %bitcast.3554, ...), kind=kLoop, calls=%fused_computation.660 | loop fusion | flops 15872 | bytes 64636 | tf_op jit(solution)/shard_map/eval_jaxpr/sub | solution.py:45
  (477 shorter events, 236.7 us)
Async XLA Ops:
  2.0 514.5 %all-to-all-start = ((f32[3,256,1,128]{3,2,0,1:T(1,128)}), f32[3,256,1,128]{3,2,0,1:T(1,128)S(1)}, u32[]{:S(2)}, u32[]{:S(2)}) async-start(f32[3,256,1,128]{3,2,0,1:T(1,128)} %copy.113), calls=%async_computation | async-start | bytes 786432 | tf_op jit(solution)/shard_map/all_to_all | solution.py:147
  15.7 489.1 %collective-permute-start = (f32[6,3,1,128]{3,1,0,2:T(4,128)S(1)}, f32[6,3,1,128]{3,1,0,2:T(4,128)S(1)}, u32[]{:S(2)}, u32[]{:S(2)}) collective-permute-start(f32[6,3,1,128]{3,1,0,2:T(4,128)S(1)} %get-tuple-element.1127), channel_id=1, source_target_pairs={{32,0},{64,32},{96,64},{128,96},{160,128},{192,160},{224,192},{256... | collective-permute-start | bytes 27656 | tf_op jit(solution)/shard_map/ppermute | solution.py:22
  25.0 479.8 %collective-permute-start.1 = (f32[6,3,1,128]{3,1,0,2:T(4,128)S(1)}, f32[6,3,1,128]{3,1,0,2:T(4,128)S(1)}, u32[]{:S(2)}, u32[]{:S(2)}) collective-permute-start(f32[6,3,1,128]{3,1,0,2:T(4,128)S(1)} %get-tuple-element.1128), channel_id=1, source_target_pairs={{0,32},{32,64},{64,96},{96,128},{128,160},{160,192},{192,224},{224... | collective-permute-start | bytes 27656 | tf_op jit(solution)/shard_map/ppermute | solution.py:19
  32.9 100.7 %copy-start.8 = (f32[3,32,128]{2,1,0:T(8,128)}, f32[3,32,128]{2,1,0:T(8,128)S(1)}, u32[]{:S(2)}) copy-start(f32[3,32,128]{2,1,0:T(8,128)S(1)} %get-tuple-element.434) | copy-start | bytes 147460
  351.3 153.5 %copy-start = (f32[3,256,1,128]{3,2,1,0:T(1,128)S(1)}, f32[3,256,1,128]{3,2,1,0:T(1,128)}, u32[]{:S(2)}) copy-start(f32[3,256,1,128]{3,2,1,0:T(1,128)} %param.13) | copy-start | bytes 1179652
  506.1 5.6 collective-permute-start.2
  512.3 64.9 %collective-permute-start.3 = (f32[6,1,1,128]{3,1,0,2:T(1,128)}, f32[6,1,1,128]{3,1,0,2:T(1,128)}, u32[]{:S(2)}, u32[]{:S(2)}) collective-permute-start(f32[6,1,1,128]{3,1,0,2:T(1,128)} %get-tuple-element.1124), channel_id=1, source_target_pairs={{32,0},{64,32},{96,64},{128,96},{160,128},{192,160},{224,192},{256... | collective-permute-start | bytes 9224 | tf_op jit(solution)/shard_map/ppermute | solution.py:22
  568.5 19.0 %all-to-all-start.1 = ((f32[32,1,3072]{2,1,0:T(1,128)}), f32[32,1,3072]{2,1,0:T(1,128)S(1)}, u32[]{:S(2)}, u32[]{:S(2)}) async-start(f32[32,1,3072]{2,1,0:T(1,128)} %reshape.854), calls=%async_computation.1 | async-start | bytes 786432 | tf_op jit(solution)/shard_map/all_to_all | solution.py:152
  601.9 19.5 %copy-start.12 = (f32[1,256]{1,0:T(1,128)S(1)}, f32[1,256]{1,0:T(1,128)}, u32[]{:S(2)}) copy-start(f32[1,256]{1,0:T(1,128)} %get-tuple-element.1191) | copy-start | bytes 3076
  601.9 19.5 %copy-start.13 = (f32[1,256]{1,0:T(1,128)S(1)}, f32[1,256]{1,0:T(1,128)}, u32[]{:S(2)}) copy-start(f32[1,256]{1,0:T(1,128)} %get-tuple-element.1192) | copy-start | bytes 3076
  601.9 19.5 %copy-start.14 = (f32[1,256]{1,0:T(1,128)S(1)}, f32[1,256]{1,0:T(1,128)}, u32[]{:S(2)}) copy-start(f32[1,256]{1,0:T(1,128)} %get-tuple-element.1193) | copy-start | bytes 3076
  601.9 19.5 %copy-start.15 = (f32[1,256]{1,0:T(1,128)S(1)}, f32[1,256]{1,0:T(1,128)}, u32[]{:S(2)}) copy-start(f32[1,256]{1,0:T(1,128)} %get-tuple-element.1194) | copy-start | bytes 3076
  601.9 19.5 %copy-start.16 = (f32[1,256]{1,0:T(1,128)S(1)}, f32[1,256]{1,0:T(1,128)}, u32[]{:S(2)}) copy-start(f32[1,256]{1,0:T(1,128)} %get-tuple-element.1195) | copy-start | bytes 3076
  601.9 19.5 %copy-start.17 = (f32[1,256]{1,0:T(1,128)S(1)}, f32[1,256]{1,0:T(1,128)}, u32[]{:S(2)}) copy-start(f32[1,256]{1,0:T(1,128)} %get-tuple-element.1196) | copy-start | bytes 3076
  601.9 19.5 %copy-start.18 = (f32[1,256]{1,0:T(1,128)S(1)}, f32[1,256]{1,0:T(1,128)}, u32[]{:S(2)}) copy-start(f32[1,256]{1,0:T(1,128)} %get-tuple-element.1197) | copy-start | bytes 3076
  601.9 19.5 %copy-start.19 = (f32[1,256]{1,0:T(1,128)S(1)}, f32[1,256]{1,0:T(1,128)}, u32[]{:S(2)}) copy-start(f32[1,256]{1,0:T(1,128)} %get-tuple-element.1198) | copy-start | bytes 3076
  601.9 19.5 %copy-start.20 = (f32[1,256]{1,0:T(1,128)S(1)}, f32[1,256]{1,0:T(1,128)}, u32[]{:S(2)}) copy-start(f32[1,256]{1,0:T(1,128)} %get-tuple-element.1199) | copy-start | bytes 3076
  602.0 19.5 %copy-start.21 = (f32[1,256]{1,0:T(1,128)S(1)}, f32[1,256]{1,0:T(1,128)}, u32[]{:S(2)}) copy-start(f32[1,256]{1,0:T(1,128)} %get-tuple-element.1169) | copy-start | bytes 3076
  602.0 19.5 %copy-start.22 = (f32[1,256]{1,0:T(1,128)S(1)}, f32[1,256]{1,0:T(1,128)}, u32[]{:S(2)}) copy-start(f32[1,256]{1,0:T(1,128)} %get-tuple-element.1170) | copy-start | bytes 3076
  602.1 38.8 %copy-start.5 = (f32[7,32,256]{2,1,0:T(8,128)S(1)}, f32[7,32,256]{2,1,0:T(8,128)}, u32[]{:S(2)}) copy-start(f32[7,32,256]{2,1,0:T(8,128)} %copy-done.4) | copy-start | bytes 688132
  614.8 26.3 %collective-permute-start.5 = (f32[3,3,1,128]{3,1,0,2:T(4,128)S(1)}, f32[3,3,1,128]{3,1,0,2:T(4,128)S(1)}, u32[]{:S(2)}, u32[]{:S(2)}) collective-permute-start(f32[3,3,1,128]{3,1,0,2:T(4,128)S(1)} %get-tuple-element.1134), channel_id=1, source_target_pairs={{0,32},{32,64},{64,96},{96,128},{128,160},{160,192},{192,224},{224... | collective-permute-start | bytes 13832 | tf_op jit(solution)/shard_map/ppermute | solution.py:19
  616.7 24.4 %collective-permute-start.4 = (f32[3,3,1,128]{3,1,0,2:T(4,128)S(1)}, f32[3,3,1,128]{3,1,0,2:T(4,128)S(1)}, u32[]{:S(2)}, u32[]{:S(2)}) collective-permute-start(f32[3,3,1,128]{3,1,0,2:T(4,128)S(1)} %get-tuple-element.1133), channel_id=1, source_target_pairs={{32,0},{64,32},{96,64},{128,96},{160,128},{192,160},{224,192},{256... | collective-permute-start | bytes 13832 | tf_op jit(solution)/shard_map/ppermute | solution.py:22
  642.0 5.5 collective-permute-start.6
  647.5 4.3 collective-permute-start.7
  (26 other events, 443.9 us)
where the time goes:
time: 661 us; the launch traced here: 653 us
  other arithmetic  457 us (69%)
  local copies, waits for them, and re-layouts  97.7 us (15%)
  starting transfers between devices  48.3 us (7%)
  loops' own time  25.7 us (4%)
  waiting for transfers between devices  11.6 us (2%)
  between operations  8.93 us (1%)
    sub x19, other arithmetic, tables(): lax.linalg.tridiagonal_solve(lower_diag, main_diag, upper_diag, identity)  379 us
    broadcast_in_dim x17, other arithmetic, tables(): lax.linalg.tridiagonal_solve(lower_diag, main_diag, upper_diag, identity)  40.6 us
    slice x110, local copies, waits for them, and re-layouts, tables(): lax.linalg.tridiagonal_solve(lower_diag, main_diag, upper_diag, identity)  35.7 us
    another operation x6, loops' own time, tables(): lax.linalg.tridiagonal_solve(lower_diag, main_diag, upper_diag, identity)  25.7 us
    unnamed x89, local copies, waits for them, and re-layouts  25.6 us
    unnamed x1, other arithmetic  22.9 us
    ppermute x4, starting transfers between devices, with_halo(): lax.ppermute(lax.slice_in_dim(block, 0, width, axis=dim), axis, backward)  21.6 us
  transfers between devices with their start and end apart: 10, of which 4 were waited for; matrix products, arithmetic and copies ran while one was open for 81% of the time, Pallas kernels for 0%

commit v1 on v0

v1 whole, which is shorter than its diff:
```python
import jax
import jax.numpy as jnp
import ml_dtypes
import numpy as np
from jax import lax
from jax.experimental import pallas as pl
from jax.experimental.pallas import tpu as pltpu
from jax.sharding import PartitionSpec as P

ALPHA_D = 1.0 / 3.0
COEF_A = 14.0 / 9.0
COEF_B = 1.0 / 9.0
ALPHA_F = 0.49
LX = 256
LZ = 128
EDGE = 96
MESH = pl.DeviceIdType.MESH


def filter_coefficients():
    return (
        (11.0 + 10.0 * ALPHA_F) / 16.0,
        (15.0 + 34.0 * ALPHA_F) / 32.0,
        (-3.0 + 6.0 * ALPHA_F) / 16.0,
        (1.0 - 2.0 * ALPHA_F) / 32.0,
    )


def line_kernel(alpha, stencil):
    root = np.sqrt(1.0 - 4.0 * alpha * alpha)
    rate = (-1.0 + root) / (2.0 * alpha)

    def response(n):
        n = np.asarray(n)
        return sum(s * rate ** np.abs(n + m) / root for m, s in stencil.items())

    far = max(stencil)
    return response, rate, float(response(far) / rate**far)


def slope_kernel():
    a, b = 0.5 * COEF_A, 0.25 * COEF_B
    response, rate, factor = line_kernel(ALPHA_D, {1: 0.5 * a, -1: -0.5 * a, 2: 0.5 * b, -2: -0.5 * b})
    return response, rate, factor, float(response(1)) - factor * rate


def smooth_kernel():
    c = filter_coefficients()
    stencil = {0: -c[0]}
    for n in (1, 2, 3):
        stencil[n] = stencil[-n] = -0.5 * c[n]
    response, rate, factor = line_kernel(ALPHA_F, stencil)
    near = [float(response(n)) - factor * rate**n for n in (1, 2)]
    return response, rate, factor, near


def halves(table):
    table = np.asarray(table, np.float32)
    high = table.astype(ml_dtypes.bfloat16)
    low = (table - high.astype(np.float32)).astype(ml_dtypes.bfloat16)
    return high, low


def tables():
    response, rate, factor, near = slope_kernel()
    i = np.arange(LX)
    k = np.arange(LZ)
    rows = np.zeros((LX + 16, LX))
    rows[:LX] = response(i[:, None] - i[None, :])
    rows[LX] = factor * rate ** (LX - i)
    rows[LX + 1] = -factor * rate ** (i + 1.0)
    slope_x = np.concatenate(halves(rows))
    high, low = halves(response(k[None, :] - k[:, None]))
    slope_z = np.block([[high, low], [high, np.zeros_like(low)]])
    sends = np.zeros((32, 6, LZ))
    for f in range(6):
        sends[f, f] = factor * rate ** (LZ - k)
        sends[6 + f, f, LZ - 1] = 1.0
        sends[16 + f, f] = -factor * rate ** (k + 1.0)
        sends[22 + f, f, 0] = 1.0
    high, low = halves(sends)
    none = np.zeros_like(low)
    send_z = np.concatenate(
        [np.concatenate([high, high], axis=2), np.concatenate([low, none], axis=2)]
    ).reshape(64, 6 * 2 * LZ)
    spread = np.zeros((32, 6, LZ))
    for f in range(6):
        spread[f, f] = rate**k
        spread[6 + f, f, 0] = near
        spread[16 + f, f] = rate ** (LZ - 1.0 - k)
        spread[22 + f, f, LZ - 1] = -near
    high, low = halves(spread.reshape(32, 6 * LZ))
    spread_z = np.concatenate([high, high, low])
    fade_x = np.zeros((2, EDGE, LZ), np.float32)
    fade_x[0] = (rate ** i[:EDGE])[:, None]
    fade_x[1] = fade_x[0, ::-1]
    response, rate, factor, _ = smooth_kernel()
    smooth_x = np.concatenate(halves(response(i[:, None] - i[None, :])))
    fade_f = np.zeros((2, LX, LZ), np.float32)
    fade_f[0] = (rate**i)[:, None]
    fade_f[1] = fade_f[0, ::-1]
    return send_z, slope_x, slope_z, spread_z, fade_x, fade_f, smooth_x


def split(values):
    high = values.astype(jnp.bfloat16)
    low = (values - high.astype(jnp.float32)).astype(jnp.bfloat16)
    return high, low


def dot(a, b, dims=((1,), (0,))):
    return lax.dot_general(a, b, (dims, ((), ())), preferred_element_type=jnp.float32)


def kernel(
    counts,
    velocity_hbm, send_z_hbm, slope_x_hbm, slope_z_hbm, spread_z_hbm, fade_x_hbm, fade_f_hbm, smooth_x_hbm,
    out_hbm,
    v, send_z, slope_x, slope_z, spread_z, fade_x, fade_f, smooth_x,
    fields, part_x, h, h_halves, out,
    z_out, z_in, x_out, x_in, f_out, f_in,
    load_sem, store_sem, send_sem, recv_sem,
):
    nx, nz = counts
    gx, gz = lax.axis_index("gx"), lax.axis_index("gz")
    x_next, x_prev = lax.rem(gx + 1, nx), lax.rem(gx + nx - 1, nx)
    z_next, z_prev = lax.rem(gz + 1, nz), lax.rem(gz + nz - 1, nz)
    sides_z = ((gx, z_next), (gx, z_prev))
    sides_x = ((x_next, gz), (x_prev, gz))

    barrier = pltpu.get_barrier_semaphore()
    for side in sides_z + sides_x:
        pl.semaphore_signal(barrier, inc=1, device_id=side, device_id_type=MESH)

    loads = [
        pltpu.make_async_copy(src, dst, load_sem.at[n])
        for n, (src, dst) in enumerate(
            (
                (velocity_hbm, v),
                (send_z_hbm, send_z),
                (slope_x_hbm, slope_x),
                (slope_z_hbm, slope_z),
                (spread_z_hbm, spread_z),
                (fade_x_hbm, fade_x),
                (fade_f_hbm, fade_f),
                (smooth_x_hbm, smooth_x),
            )
        )
    ]
    for load in loads:
        load.start()

    loads[0].wait()
    u, w = v[0], v[2]
    for n, field in enumerate((u * u, u * v[1], u, v[1], w, u * w, w * v[1], w * w)):
        high, low = split(field)
        fields[:, n * 256 : n * 256 + 128] = high
        fields[:, n * 256 + 128 : n * 256 + 256] = low

    loads[1].wait()
    both = dot(send_z[...], fields[:, 512:], ((1,), (1,)))
    z_out[...] = both[:32] + both[32:]
    pl.semaphore_wait(barrier, 4)
    copies_z = []
    for n, side in enumerate(sides_z):
        copies_z.append(
            pltpu.make_async_remote_copy(
                src_ref=z_out.at[pl.ds(16 * n, 16)],
                dst_ref=z_in.at[pl.ds(16 * n, 16)],
                send_sem=send_sem.at[n],
                recv_sem=recv_sem.at[n],
                device_id=side,
                device_id_type=MESH,
            )
        )
        copies_z[-1].start()

    loads[2].wait()
    for f in range(6):
        full = dot(slope_x[...], fields[:, f * 256 : f * 256 + 256])
        part = full[: LX + 16, :128] + full[: LX + 16, 128:] + full[LX + 16 :, :128]
        part_x[f] = part[:LX]
        x_out[0, f : f + 1] = part[LX : LX + 1]
        x_out[1, f : f + 1] = part[LX + 1 : LX + 2]
    for side, row in ((0, LX - 1), (1, 0)):
        ur, vr, wr = v[0, row : row + 1], v[1, row : row + 1], v[2, row : row + 1]
        for f, value in enumerate((ur * ur, ur * vr, ur, vr, wr, ur * wr)):
            x_out[side, 6 + f : 7 + f] = value
    copies_x = []
    for n, side in enumerate(sides_x):
        copies_x.append(
            pltpu.make_async_remote_copy(
                src_ref=x_out.at[n],
                dst_ref=x_in.at[n],
                send_sem=send_sem.at[2 + n],
                recv_sem=recv_sem.at[2 + n],
                device_id=side,
                device_id_type=MESH,
            )
        )
        copies_x[-1].start()

    loads[3].wait()
    flat = (0, 1, 5)
    for c in range(3):
        total = part_x[flat[c]] + u * part_x[2 + c]
        for f, factor in ((2 + c, w), (5 + c, None)):
            full = dot(fields[:, f * 256 : f * 256 + 256], slope_z[...])
            part = full[:, :128] + full[:, 128:]
            total = total + (part if factor is None else factor * part)
        h[c] = total

    for load in loads[4:]:
        load.wait()
    _, _, _, near_d = slope_kernel()
    first = lax.broadcasted_iota(jnp.int32, (8, LZ), 0) == 0
    last = lax.broadcasted_iota(jnp.int32, (8, LZ), 0) == 7
    for copy in copies_x:
        copy.wait()
    for c in range(3):
        uv, vc = flat[c], 2 + c
        rows = slice(0, EDGE)
        h[c, rows] += fade_x[0] * (x_in[0, uv : uv + 1] + v[0, rows] * x_in[0, vc : vc + 1])
        near = x_in[0, 6 + uv : 7 + uv] + v[0, 0:8] * x_in[0, 6 + vc : 7 + vc]
        h[c, 0:8] += jnp.where(first, near_d * near, 0.0)
        rows = slice(LX - EDGE, LX)
        h[c, rows] += fade_x[1] * (x_in[1, uv : uv + 1] + v[0, rows] * x_in[1, vc : vc + 1])
        near = x_in[1, 6 + uv : 7 + uv] + v[0, LX - 8 : LX] * x_in[1, 6 + vc : 7 + vc]
        h[c, LX - 8 : LX] -= jnp.where(last, near_d * near, 0.0)

    for copy in copies_z:
        copy.wait()
    high, low = split(z_in[...])
    spread = dot(jnp.concatenate([high, low, high]), spread_z[...], ((0,), (0,)))
    for c in range(3):
        at, to = (3 + c) * 128, c * 128
        h[c] += spread[:, at : at + 128] + w * spread[:, to : to + 128]

    for c in range(3):
        for side, (a, b) in enumerate(((LX - 1, LX - 2), (0, 1))):
            f_out[side, c : c + 1] = jnp.sum(fade_f[1 - side] * h[c], axis=0, keepdims=True)
            f_out[side, 3 + c : 4 + c] = h[c, a : a + 1]
            f_out[side, 6 + c : 7 + c] = h[c, b : b + 1]
    copies_f = []
    for n, side in enumerate(sides_x):
        copies_f.append(
            pltpu.make_async_remote_copy(
                src_ref=f_out.at[n],
                dst_ref=f_in.at[n],
                send_sem=send_sem.at[4 + n],
                recv_sem=recv_sem.at[4 + n],
                device_id=side,
                device_id_type=MESH,
            )
        )
        copies_f[-1].start()

    for c in range(3):
        high, low = split(h[c])
        h_halves[c, :, :128] = high
        h_halves[c, :, 128:] = low
        full = dot(smooth_x[...], h_halves[c])
        out[c] = full[:LX, :128] + full[:LX, 128:] + full[LX:, :128]

    _, rate, factor, (near1, near2) = smooth_kernel()
    row = lax.broadcasted_iota(jnp.int32, (8, LZ), 0)
    for copy in copies_f:
        copy.wait()
    stores = []
    for c in range(3):
        scale = rate * factor
        below, above = scale * f_in[0, c : c + 1], scale * f_in[1, c : c + 1]
        out[c] += fade_f[0] * below + fade_f[1] * above
        for side, start, end0, end1 in ((0, 0, 0, 1), (1, LX - 8, 7, 6)):
            cell1, cell2 = f_in[side, 3 + c : 4 + c], f_in[side, 6 + c : 7 + c]
            out[c, start : start + 8] += jnp.where(row == end0, near1 * cell1 + near2 * cell2, 0.0) + jnp.where(
                row == end1, near2 * cell1, 0.0
            )
        stores.append(pltpu.make_async_copy(out.at[c], out_hbm.at[c], store_sem.at[c]))
        stores[-1].start()
    for store in stores:
        store.wait()


def per_device(counts, velocity):
    operands = [jnp.asarray(t) for t in tables()]
    bf16, f32 = jnp.bfloat16, jnp.float32
    flat = velocity.reshape(3, LX, LZ)
    out = pl.pallas_call(
        lambda *refs: kernel(counts, *refs),
        out_shape=jax.ShapeDtypeStruct((3, LX, LZ), f32),
        in_specs=[pl.BlockSpec(memory_space=pl.ANY)] * 8,
        out_specs=pl.BlockSpec(memory_space=pl.ANY),
        scratch_shapes=[pltpu.VMEM((3, LX, LZ), f32)]
        + [pltpu.VMEM(t.shape, t.dtype) for t in operands]
        + [
            pltpu.VMEM((LX, 8 * 256), bf16),
            pltpu.VMEM((6, LX, LZ), f32),
            pltpu.VMEM((3, LX, LZ), f32),
            pltpu.VMEM((3, LX, 2 * LZ), bf16),
            pltpu.VMEM((3, LX, LZ), f32),
            pltpu.VMEM((32, LX), f32),
            pltpu.VMEM((32, LX), f32),
            pltpu.VMEM((2, 16, LZ), f32),
            pltpu.VMEM((2, 16, LZ), f32),
            pltpu.VMEM((2, 16, LZ), f32),
            pltpu.VMEM((2, 16, LZ), f32),
            pltpu.SemaphoreType.DMA((8,)),
            pltpu.SemaphoreType.DMA((3,)),
            pltpu.SemaphoreType.DMA((6,)),
            pltpu.SemaphoreType.DMA((6,)),
        ],
        compiler_params=pltpu.CompilerParams(collective_id=0, has_side_effects=True, vmem_limit_bytes=32 * 2**20),
    )(flat, *operands)
    return out.reshape(3, LX, 1, LZ)


def solution(mesh):
    counts = (mesh.shape["gx"], mesh.shape["gz"])
    return jax.shard_map(
        lambda velocity: per_device(counts, velocity),
        mesh=mesh,
        in_specs=(P(None, "gx", None, "gz"),),
        out_specs=P(None, "gx", None, "gz"),
        check_vma=False,
    )
```

time: 661 us -> 28.8 us (0.04)
  the two profiles are of different devices: /device:TPU:1 before, /device:TPU:32 now
where the time goes in v1:
time: 28.8 us; the launch traced here: 28.4 us
  Pallas kernels  20.2 us (70%)
  local copies, waits for them, and re-layouts  8.23 us (29%)
    pallas_call x1, Pallas kernels, per_device(): pl.pallas_call(lambda *refs: kernel(counts, *refs), out_shape=jax.ShapeDt...  20.2 us
    unnamed x17, local copies, waits for them, and re-layouts  8.23 us

profile of v1, /device:TPU:32, one launch (start us, length us, event | category | flops | bytes accessed | tf_op | source)
XLA Modules:
  0.0 28.4 jit_solution(17377611523646621171)
XLA Ops:
  0.0 0.0 copy-start
  0.0 1.0 %copy-done = f32[3,256,1,128]{3,2,1,0:T(1,128)S(1)} copy-done((f32[3,256,1,128]{3,2,1,0:T(1,128)S(1)}, f32[3,256,1,128]{3,2,1,0:T(1,128)}, u32[]{:S(2)}) %copy-start) | copy-done | bytes 393240
  1.0 0.0 copy-start.1
  1.0 1.0 %copy-done.1 = bf16[544,256]{1,0:T(8,128)(2,1)S(1)} copy-done((bf16[544,256]{1,0:T(8,128)(2,1)S(1)}, bf16[544,256]{1,0:T(8,128)(2,1)}, u32[]{:S(2)}) %copy-start.1) | copy-done | bytes 278552
  2.0 0.0 copy-start.2
  2.0 0.9 %copy-done.2 = bf16[512,256]{1,0:T(8,128)(2,1)S(1)} copy-done((bf16[512,256]{1,0:T(8,128)(2,1)S(1)}, bf16[512,256]{1,0:T(8,128)(2,1)}, u32[]{:S(2)}) %copy-start.2) | copy-done | bytes 262168
  2.9 0.0 copy-start.3
  2.9 0.9 %copy-done.3 = f32[2,256,128]{2,1,0:T(8,128)S(1)} copy-done((f32[2,256,128]{2,1,0:T(8,128)S(1)}, f32[2,256,128]{2,1,0:T(8,128)}, u32[]{:S(2)}) %copy-start.3) | copy-done | bytes 262168
  3.9 0.0 copy-start.4
  3.9 0.9 %copy-done.4 = bf16[64,1536]{1,0:T(8,128)(2,1)S(1)} copy-done((bf16[64,1536]{1,0:T(8,128)(2,1)S(1)}, bf16[64,1536]{1,0:T(8,128)(2,1)}, u32[]{:S(2)}) %copy-start.4) | copy-done | bytes 196632
  4.8 0.0 copy-start.5
  4.8 0.9 %copy-done.5 = bf16[96,768]{1,0:T(8,128)(2,1)S(1)} copy-done((bf16[96,768]{1,0:T(8,128)(2,1)S(1)}, bf16[96,768]{1,0:T(8,128)(2,1)}, u32[]{:S(2)}) %copy-start.5) | copy-done | bytes 147480
  5.7 0.0 copy-start.6
  5.7 0.9 %copy-done.6 = bf16[256,256]{1,0:T(8,128)(2,1)S(1)} copy-done((bf16[256,256]{1,0:T(8,128)(2,1)S(1)}, bf16[256,256]{1,0:T(8,128)(2,1)}, u32[]{:S(2)}) %copy-start.6) | copy-done | bytes 131096
  6.6 0.0 copy-start.7
  6.6 0.9 %copy-done.7 = f32[2,96,128]{2,1,0:T(8,128)S(1)} copy-done((f32[2,96,128]{2,1,0:T(8,128)S(1)}, f32[2,96,128]{2,1,0:T(8,128)}, u32[]{:S(2)}) %copy-start.7) | copy-done | bytes 98328
  7.5 20.2 %shard_map.82 = f32[3,256,128]{2,1,0:T(8,128)S(1)} custom-call(f32[3,256,128]{2,1,0:T(8,128)S(1)} %bitcast.5, bf16[64,1536]{1,0:T(8,128)(2,1)S(1)} %copy-done.4, bf16[544,256]{1,0:T(8,128)(2,1)S(1)} %copy-done.1, bf16[256,256]{1,0:T(8,128)(2,1)S(1)} %copy-done.6, bf16[96,768]{1,0:T(8,128)(2,1)S(1)} %copy-done.5, f32[2,96,128]{2,1,0:T(8,128)S(1)} %copy-done.7, ...), custom_call_target="tpu_custom_call" | custom-call | tf_op jit(solution)/shard_map/pallas_call | solution.py:289
  27.7 0.7 %copy.11 = f32[3,256,1,128]{3,2,1,0:T(1,128)} copy(f32[3,256,1,128]{3,2,1,0:T(1,128)S(1)} %bitcast.4) | data formatting | bytes 786432
Async XLA Ops:
  0.0 1.0 %copy-start = (f32[3,256,1,128]{3,2,1,0:T(1,128)S(1)}, f32[3,256,1,128]{3,2,1,0:T(1,128)}, u32[]{:S(2)}) copy-start(f32[3,256,1,128]{3,2,1,0:T(1,128)} %param.8) | copy-start | bytes 1179652
  1.0 1.0 %copy-start.1 = (bf16[544,256]{1,0:T(8,128)(2,1)S(1)}, bf16[544,256]{1,0:T(8,128)(2,1)}, u32[]{:S(2)}) copy-start(bf16[544,256]{1,0:T(8,128)(2,1)} %constant.15.clone.refs_2_) | copy-start | bytes 835588
  2.0 0.9 %copy-start.2 = (bf16[512,256]{1,0:T(8,128)(2,1)S(1)}, bf16[512,256]{1,0:T(8,128)(2,1)}, u32[]{:S(2)}) copy-start(bf16[512,256]{1,0:T(8,128)(2,1)} %constant.20.clone.refs_7_) | copy-start | bytes 786436
  2.9 0.9 %copy-start.3 = (f32[2,256,128]{2,1,0:T(8,128)S(1)}, f32[2,256,128]{2,1,0:T(8,128)}, u32[]{:S(2)}) copy-start(f32[2,256,128]{2,1,0:T(8,128)} %constant.19.clone.refs_6_) | copy-start | bytes 786436
  3.9 0.9 %copy-start.4 = (bf16[64,1536]{1,0:T(8,128)(2,1)S(1)}, bf16[64,1536]{1,0:T(8,128)(2,1)}, u32[]{:S(2)}) copy-start(bf16[64,1536]{1,0:T(8,128)(2,1)} %constant.14.clone.refs_1_) | copy-start | bytes 589828
  4.8 0.9 %copy-start.5 = (bf16[96,768]{1,0:T(8,128)(2,1)S(1)}, bf16[96,768]{1,0:T(8,128)(2,1)}, u32[]{:S(2)}) copy-start(bf16[96,768]{1,0:T(8,128)(2,1)} %constant.17.clone.refs_4_) | copy-start | bytes 442372
  5.7 0.9 %copy-start.6 = (bf16[256,256]{1,0:T(8,128)(2,1)S(1)}, bf16[256,256]{1,0:T(8,128)(2,1)}, u32[]{:S(2)}) copy-start(bf16[256,256]{1,0:T(8,128)(2,1)} %constant.16.clone.refs_3_) | copy-start | bytes 393220
  6.6 0.9 %copy-start.7 = (f32[2,96,128]{2,1,0:T(8,128)S(1)}, f32[2,96,128]{2,1,0:T(8,128)}, u32[]{:S(2)}) copy-start(f32[2,96,128]{2,1,0:T(8,128)} %constant.18.clone.refs_5_) | copy-start | bytes 294916

commit v2 on v1

--- a/solution.py
+++ b/solution.py
@@ -115,11 +115,11 @@
 def kernel(
     counts,
     velocity_hbm, send_z_hbm, slope_x_hbm, slope_z_hbm, spread_z_hbm, fade_x_hbm, fade_f_hbm, smooth_x_hbm,
-    out_hbm,
+    out,
     v, send_z, slope_x, slope_z, spread_z, fade_x, fade_f, smooth_x,
-    fields, part_x, h, h_halves, out,
+    fields, part_x, h, h_halves,
     z_out, z_in, x_out, x_in, f_out, f_in,
-    load_sem, store_sem, send_sem, recv_sem,
+    load_sem, send_sem, recv_sem,
 ):
     nx, nz = counts
     gx, gz = lax.axis_index("gx"), lax.axis_index("gz")
@@ -266,7 +266,6 @@
     row = lax.broadcasted_iota(jnp.int32, (8, LZ), 0)
     for copy in copies_f:
         copy.wait()
-    stores = []
     for c in range(3):
         scale = rate * factor
         below, above = scale * f_in[0, c : c + 1], scale * f_in[1, c : c + 1]
@@ -276,21 +275,17 @@
             out[c, start : start + 8] += jnp.where(row == end0, near1 * cell1 + near2 * cell2, 0.0) + jnp.where(
                 row == end1, near2 * cell1, 0.0
             )
-        stores.append(pltpu.make_async_copy(out.at[c], out_hbm.at[c], store_sem.at[c]))
-        stores[-1].start()
-    for store in stores:
-        store.wait()
 
 
 def per_device(counts, velocity):
-    operands = [jnp.asarray(t) for t in tables()]
+    operands = [pltpu.with_memory_space_constraint(jnp.asarray(t), pltpu.HBM) for t in tables()]
     bf16, f32 = jnp.bfloat16, jnp.float32
-    flat = velocity.reshape(3, LX, LZ)
+    flat = pltpu.with_memory_space_constraint(velocity.reshape(3, LX, LZ), pltpu.HBM)
     out = pl.pallas_call(
         lambda *refs: kernel(counts, *refs),
         out_shape=jax.ShapeDtypeStruct((3, LX, LZ), f32),
-        in_specs=[pl.BlockSpec(memory_space=pl.ANY)] * 8,
-        out_specs=pl.BlockSpec(memory_space=pl.ANY),
+        in_specs=[pl.BlockSpec(memory_space=pltpu.HBM)] * 8,
+        out_specs=pl.BlockSpec(memory_space=pltpu.VMEM),
         scratch_shapes=[pltpu.VMEM((3, LX, LZ), f32)]
         + [pltpu.VMEM(t.shape, t.dtype) for t in operands]
         + [
@@ -298,7 +293,6 @@
             pltpu.VMEM((6, LX, LZ), f32),
             pltpu.VMEM((3, LX, LZ), f32),
             pltpu.VMEM((3, LX, 2 * LZ), bf16),
-            pltpu.VMEM((3, LX, LZ), f32),
             pltpu.VMEM((32, LX), f32),
             pltpu.VMEM((32, LX), f32),
             pltpu.VMEM((2, 16, LZ), f32),
@@ -306,7 +300,6 @@
             pltpu.VMEM((2, 16, LZ), f32),
             pltpu.VMEM((2, 16, LZ), f32),
             pltpu.SemaphoreType.DMA((8,)),
-            pltpu.SemaphoreType.DMA((3,)),
             pltpu.SemaphoreType.DMA((6,)),
             pltpu.SemaphoreType.DMA((6,)),
         ],

time: 28.8 us -> 20.5 us (0.71)
  local copies, waits for them, and re-layouts: 8.23 us -> 0.75 us
  Pallas kernels: 20.2 us -> 19.6 us
    unnamed x17 -> x1, local copies, waits for them, and re-layouts: 8.23 us -> 0.75 us
    pallas_call x1, Pallas kernels: 20.2 us -> 19.6 us  [per_device(): pl.pallas_call(lambda *refs: kernel(counts, *refs), out_shape=jax.ShapeDt...]
where the time goes in v2:
time: 20.5 us; the launch traced here: 20.3 us
  Pallas kernels  19.6 us (96%)
  local copies, waits for them, and re-layouts  0.75 us (4%)
    pallas_call x1, Pallas kernels, per_device(): pl.pallas_call(lambda *refs: kernel(counts, *refs), out_shape=jax.ShapeDt...  19.6 us
    unnamed x1, local copies, waits for them, and re-layouts  0.75 us

profile of v2, /device:TPU:32, one launch (start us, length us, event | category | flops | bytes accessed | tf_op | source)
XLA Modules:
  0.0 20.3 jit_solution(1759584351898524033)
XLA Ops:
  0.0 19.6 %shard_map.82 = f32[3,256,128]{2,1,0:T(8,128)S(1)} custom-call(f32[3,256,128]{2,1,0:T(8,128)} %bitcast.5, bf16[64,1536]{1,0:T(8,128)(2,1)} %constant.14.clone.refs_1_, bf16[544,256]{1,0:T(8,128)(2,1)} %constant.15.clone.refs_2_, bf16[256,256]{1,0:T(8,128)(2,1)} %constant.16.clone.refs_3_, bf16[96,768]{1,0:T(8,128)(2,1)} %constant.17.clone.refs_4_, ...), custom_call_target="tpu_custom_call" | custom-call | tf_op jit(solution)/shard_map/pallas_call | solution.py:284
  19.6 0.7 %copy.11 = f32[3,256,1,128]{3,2,1,0:T(1,128)} copy(f32[3,256,1,128]{3,2,1,0:T(1,128)S(1)} %bitcast.4) | data formatting | bytes 786432

commit v3 on v2

v3 whole, which is shorter than its diff:
```python
import jax
import jax.numpy as jnp
import ml_dtypes
import numpy as np
from jax import lax
from jax.experimental import pallas as pl
from jax.experimental.pallas import tpu as pltpu
from jax.sharding import PartitionSpec as P

ALPHA_D = 1.0 / 3.0
COEF_A = 14.0 / 9.0
COEF_B = 1.0 / 9.0
ALPHA_F = 0.49
LX = 256
LZ = 128
EDGE = 96
EARLY = 3
MESH = pl.DeviceIdType.MESH


def filter_coefficients():
    return (
        (11.0 + 10.0 * ALPHA_F) / 16.0,
        (15.0 + 34.0 * ALPHA_F) / 32.0,
        (-3.0 + 6.0 * ALPHA_F) / 16.0,
        (1.0 - 2.0 * ALPHA_F) / 32.0,
    )


def line_kernel(alpha, stencil):
    root = np.sqrt(1.0 - 4.0 * alpha * alpha)
    rate = (-1.0 + root) / (2.0 * alpha)

    def response(n):
        n = np.asarray(n)
        return sum(s * rate ** np.abs(n + m) / root for m, s in stencil.items())

    far = max(stencil)
    return response, rate, float(response(far) / rate**far)


def slope_kernel():
    a, b = 0.5 * COEF_A, 0.25 * COEF_B
    response, rate, factor = line_kernel(ALPHA_D, {1: 0.5 * a, -1: -0.5 * a, 2: 0.5 * b, -2: -0.5 * b})
    return response, rate, factor, float(response(1)) - factor * rate


def smooth_kernel():
    c = filter_coefficients()
    stencil = {0: -c[0]}
    for n in (1, 2, 3):
        stencil[n] = stencil[-n] = -0.5 * c[n]
    response, rate, factor = line_kernel(ALPHA_F, stencil)
    near = [float(response(n)) - factor * rate**n for n in (1, 2)]
    return response, rate, factor, near


def halves(table):
    table = np.asarray(table, np.float32)
    high = table.astype(ml_dtypes.bfloat16)
    low = (table - high.astype(np.float32)).astype(ml_dtypes.bfloat16)
    return high, low


def tables():
    response, rate, factor, near = slope_kernel()
    i = np.arange(LX)
    k = np.arange(LZ)
    slope_x = np.concatenate(halves(response(i[:, None] - i[None, :])))
    high, low = halves(response(k[None, :] - k[:, None]))
    slope_z = np.block([[high, low], [high, np.zeros_like(low)]])
    sends = np.zeros((8, LZ))
    sends[0] = factor * rate ** (LZ - k)
    sends[1, LZ - 1] = 1.0
    sends[2] = -factor * rate ** (k + 1.0)
    sends[3, 0] = 1.0
    high, low = halves(sends)
    send_z = np.block([[high, high], [low, np.zeros_like(low)]])
    spread = np.zeros((32, 6, LZ))
    for f in range(6):
        spread[2 * f, f] = rate**k
        spread[2 * f + 1, f, 0] = near
        spread[16 + 2 * f, f] = rate ** (LZ - 1.0 - k)
        spread[17 + 2 * f, f, LZ - 1] = -near
    high, low = halves(spread.reshape(32, 6 * LZ))
    spread_z = np.concatenate([high, high, low])
    fade_x = np.zeros((2, EDGE, LZ), np.float32)
    fade_x[0] = (rate ** i[:EDGE])[:, None]
    fade_x[1] = fade_x[0, ::-1]
    response, rate, factor, _ = smooth_kernel()
    smooth_x = np.concatenate(halves(response(i[:, None] - i[None, :])))
    fade_f = np.zeros((2, LX, LZ), np.float32)
    fade_f[0] = (rate**i)[:, None]
    fade_f[1] = fade_f[0, ::-1]
    return fade_x, send_z, slope_x, slope_z, spread_z, fade_f, smooth_x


def split(values):
    high = values.astype(jnp.bfloat16)
    low = (values - high.astype(jnp.float32)).astype(jnp.bfloat16)
    return high, low


def dot(a, b, dims=((1,), (0,))):
    return lax.dot_general(a, b, (dims, ((), ())), preferred_element_type=jnp.float32)


def total(values):
    return jnp.sum(values, axis=0, keepdims=True)


def kernel(
    counts,
    velocity_hbm, fade_x_hbm, send_z_hbm, slope_x_hbm, slope_z_hbm, spread_z_hbm, fade_f_hbm, smooth_x_hbm,
    out,
    v, fade_x, send_z, slope_x, slope_z, spread_z, fade_f, smooth_x,
    fields, part_x, h, h_halves,
    z_out, z_in, x_out, x_in, f_out, f_in,
    load_sem, send_sem, recv_sem, ready,
):
    nx, nz = counts
    gx, gz = lax.axis_index("gx"), lax.axis_index("gz")
    x_next, x_prev = lax.rem(gx + 1, nx), lax.rem(gx + nx - 1, nx)
    z_next, z_prev = lax.rem(gz + 1, nz), lax.rem(gz + nz - 1, nz)
    sides_z = ((gx, z_next), (gx, z_prev))
    sides_x = ((x_next, gz), (x_prev, gz))
    is_first, is_last = gx == 0, gx == nx - 1

    def signal(semaphore, side):
        pl.semaphore_signal(semaphore, inc=1, device_id=side, device_id_type=MESH)

    def remote(source, target, n, side):
        return pltpu.make_async_remote_copy(
            src_ref=source,
            dst_ref=target,
            send_sem=send_sem.at[n],
            recv_sem=recv_sem.at[n],
            device_id=side,
            device_id_type=MESH,
        )

    loads = [
        pltpu.make_async_copy(src, dst, load_sem.at[n])
        for n, (src, dst) in enumerate(
            (
                (velocity_hbm, v),
                (fade_x_hbm, fade_x),
                (send_z_hbm, send_z),
                (slope_x_hbm, slope_x),
                (slope_z_hbm, slope_z),
                (spread_z_hbm, spread_z),
                (fade_f_hbm, fade_f),
                (smooth_x_hbm, smooth_x),
            )
        )
    ]
    for load in loads[:EARLY]:
        load.start()

    barrier = pltpu.get_barrier_semaphore()
    for side in sides_z + (sides_x[1],):
        signal(barrier, side)

    @pl.when(jnp.logical_not(is_last))
    def _():
        signal(barrier, sides_x[0])

    z_out[...] = jnp.zeros_like(z_out)
    for load in loads[:3]:
        load.wait()
    for load in loads[EARLY:]:
        load.start()
    u, w = v[0], v[2]
    values = (u * u, u * v[1], u, v[1], w, u * w, w * v[1], w * w)
    for n in (2, 3, 4, 5, 6, 7, 0, 1):
        high, low = split(values[n])
        fields[:, n * 256 : n * 256 + 128] = high
        fields[:, n * 256 + 128 : n * 256 + 256] = low

    for f in range(6):
        both = dot(send_z[...], fields[:, (2 + f) * 256 : (3 + f) * 256], ((1,), (1,)))
        both = both[:8] + both[8:]
        z_out[2 * f : 2 * f + 2] = both[0:2]
        z_out[16 + 2 * f : 18 + 2 * f] = both[2:4]

    rate_d, factor_d, near_d = slope_kernel()[1:]
    for side, row in ((0, LX - 1), (1, 0)):
        rows = slice(LX - EDGE, LX) if side == 0 else slice(0, EDGE)
        scale = factor_d * rate_d if side == 0 else -factor_d * rate_d
        for f in range(6):
            x_out[side, f : f + 1] = scale * total(fade_x[1 - side] * values[f][rows])
            x_out[side, 6 + f : 7 + f] = values[f][row : row + 1]

    pl.semaphore_wait(barrier, jnp.where(is_first, 3, 4))
    copies = [remote(z_out.at[pl.ds(16 * n, 16)], z_in.at[pl.ds(16 * n, 16)], n, sides_z[n]) for n in (0, 1)]
    copies += [remote(x_out.at[n], x_in.at[n], 2 + n, sides_x[n]) for n in (0, 1)]
    copies += [remote(f_out.at[n], f_in.at[n], 4 + n, sides_x[n]) for n in (0, 1)]
    for n in (0, 1, 2):
        copies[n].start()

    @pl.when(is_last)
    def _():
        signal(ready, sides_x[0])

    @pl.when(jnp.logical_not(is_first))
    def _():
        copies[3].start()

    loads[3].wait()
    loads[4].wait()
    flat = (0, 1, 5)
    for f in range(6):
        full = dot(slope_x[...], fields[:, f * 256 : f * 256 + 256])
        part_x[f] = full[:LX, :128] + full[:LX, 128:] + full[LX:, :128]
    for c in range(3):
        value = part_x[flat[c]] + v[0] * part_x[2 + c]
        for f, by_w in ((2 + c, True), (5 + c, False)):
            full = dot(fields[:, f * 256 : f * 256 + 256], slope_z[...])
            part = full[:, :128] + full[:, 128:]
            value = value + (v[2] * part if by_w else part)
        h[c] = value

    for load in loads[5:]:
        load.wait()

    top, end = slice(0, EDGE), slice(LX - EDGE, LX)
    f_out[0, 9:10] = total(fade_f[1, end] * (fade_x[1] * v[0, end]))
    f_out[0, 10:11] = v[0, LX - 1 : LX]
    f_out[0, 11:12] = v[0, LX - 2 : LX - 1]
    f_out[1, 9:10] = total(fade_f[0, top] * (fade_x[0] * v[0, top]))
    f_out[1, 10:11] = v[0, 0:1]
    f_out[1, 11:12] = v[0, 1:2]
    far = (
        total(fade_f[1, top] * (fade_x[0] * v[0, top])),
        total(fade_f[0, end] * (fade_x[1] * v[0, end])),
    )
    rate_f, factor_f, (near1, near2) = smooth_kernel()[1:]
    powers = np.arange(EDGE, dtype=np.float64)
    near_sum = float(np.sum((rate_f * rate_d) ** powers))
    far_sum = float(np.sum(rate_f ** (LX - 1 - powers) * rate_d**powers))
    far_end = float(rate_f ** (LX - 1))

    @pl.when(is_first)
    def _():
        pl.semaphore_wait(ready, 1)
        copies[3].start()

    copies[0].wait_recv()
    copies[1].wait_recv()
    high, low = split(z_in[...])
    spread = dot(jnp.concatenate([high, low, high]), spread_z[...], ((0,), (0,)))
    ends = []
    for c in range(3):
        at, to = (3 + c) * 128, c * 128
        value = h[c] + (spread[:, at : at + 128] + v[2] * spread[:, to : to + 128])
        h[c] = value
        ends.append((total(fade_f[1] * value), total(fade_f[0] * value)))

    first = lax.broadcasted_iota(jnp.int32, (8, LZ), 0) == 0
    last = lax.broadcasted_iota(jnp.int32, (8, LZ), 0) == 7
    for side, (edge, row0, row1) in enumerate(((0, LX - 1, LX - 2), (LX - 1, 0, 1))):
        copies[2 + side].wait_recv()
        sign = near_d if side == 0 else -near_d
        for c in range(3):
            uv, vc = flat[c], 2 + c
            from_far = far_sum * x_in[side, uv : uv + 1] + far[side] * x_in[side, vc : vc + 1]
            cell = x_in[side, 6 + uv : 7 + uv] + v[0, edge : edge + 1] * x_in[side, 6 + vc : 7 + vc]
            f_out[side, c : c + 1] = ends[c][side] + from_far + (sign * far_end) * cell
            f_out[side, 3 + c : 4 + c] = h[c, row0 : row0 + 1]
            f_out[side, 6 + c : 7 + c] = h[c, row1 : row1 + 1]
        copies[4 + side].start()

    for c in range(3):
        uv, vc = flat[c], 2 + c
        h[c, top] += fade_x[0] * (x_in[0, uv : uv + 1] + v[0, top] * x_in[0, vc : vc + 1])
        cell = x_in[0, 6 + uv : 7 + uv] + v[0, 0:8] * x_in[0, 6 + vc : 7 + vc]
        h[c, 0:8] += jnp.where(first, near_d * cell, 0.0)
        h[c, end] += fade_x[1] * (x_in[1, uv : uv + 1] + v[0, end] * x_in[1, vc : vc + 1])
        cell = x_in[1, 6 + uv : 7 + uv] + v[0, LX - 8 : LX] * x_in[1, 6 + vc : 7 + vc]
        h[c, LX - 8 : LX] -= jnp.where(last, near_d * cell, 0.0)

    for c in range(3):
        high, low = split(h[c])
        h_halves[c, :, :128] = high
        h_halves[c, :, 128:] = low
        full = dot(smooth_x[...], h_halves[c])
        out[c] = full[:LX, :128] + full[:LX, 128:] + full[LX:, :128]

    row = lax.broadcasted_iota(jnp.int32, (8, LZ), 0)
    copies[5].wait_recv()
    copies[4].wait_recv()
    scale = rate_f * factor_f
    for c in range(3):
        uv, vc = flat[c], 2 + c
        sums = []
        for side, sign, start, end0, end1 in ((0, -near_d, 0, 0, 1), (1, near_d, LX - 8, 7, 6)):
            own, own_v = x_out[1 - side, uv : uv + 1], x_out[1 - side, vc : vc + 1]
            edge, edge_v = x_out[1 - side, 6 + uv : 7 + uv], x_out[1 - side, 6 + vc : 7 + vc]
            moment, u1, u2 = (f_in[side, n : n + 1] for n in (9, 10, 11))
            cell = sign * (edge + u1 * edge_v)
            sums.append(scale * (f_in[side, c : c + 1] + near_sum * own + moment * own_v + cell))
            cell1 = f_in[side, 3 + c : 4 + c] + own + u1 * own_v + cell
            cell2 = f_in[side, 6 + c : 7 + c] + rate_d * (own + u2 * own_v)
            out[c, start : start + 8] += jnp.where(row == end0, near1 * cell1 + near2 * cell2, 0.0) + jnp.where(
                row == end1, near2 * cell1, 0.0
            )
        out[c] += fade_f[0] * sums[0] + fade_f[1] * sums[1]
    for copy in copies:
        copy.wait_send()


def per_device(counts, velocity):
    operands = [pltpu.with_memory_space_constraint(jnp.asarray(t), pltpu.HBM) for t in tables()]
    bf16, f32 = jnp.bfloat16, jnp.float32
    flat = pltpu.with_memory_space_constraint(velocity.reshape(3, LX, LZ), pltpu.HBM)
    out = pl.pallas_call(
        lambda *refs: kernel(counts, *refs),
        out_shape=jax.ShapeDtypeStruct((3, LX, LZ), f32),
        in_specs=[pl.BlockSpec(memory_space=pltpu.HBM)] * 8,
        out_specs=pl.BlockSpec(memory_space=pltpu.VMEM),
        scratch_shapes=[pltpu.VMEM((3, LX, LZ), f32)]
        + [pltpu.VMEM(t.shape, t.dtype) for t in operands]
        + [
            pltpu.VMEM((LX, 8 * 256), bf16),
            pltpu.VMEM((6, LX, LZ), f32),
            pltpu.VMEM((3, LX, LZ), f32),
            pltpu.VMEM((3, LX, 2 * LZ), bf16),
            pltpu.VMEM((32, LX), f32),
            pltpu.VMEM((32, LX), f32),
            pltpu.VMEM((2, 16, LZ), f32),
            pltpu.VMEM((2, 16, LZ), f32),
            pltpu.VMEM((2, 16, LZ), f32),
            pltpu.VMEM((2, 16, LZ), f32),
            pltpu.SemaphoreType.DMA((8,)),
            pltpu.SemaphoreType.DMA((6,)),
            pltpu.SemaphoreType.DMA((6,)),
            pltpu.SemaphoreType.REGULAR,
        ],
        compiler_params=pltpu.CompilerParams(collective_id=0, has_side_effects=True, vmem_limit_bytes=32 * 2**20),
    )(flat, *operands)
    return out.reshape(3, LX, 1, LZ)


def solution(mesh):
    counts = (mesh.shape["gx"], mesh.shape["gz"])
    return jax.shard_map(
        lambda velocity: per_device(counts, velocity),
        mesh=mesh,
        in_specs=(P(None, "gx", None, "gz"),),
        out_specs=P(None, "gx", None, "gz"),
        check_vma=False,
    )
```

time: 20.5 us -> 19.4 us (0.946)
  the two profiles are of different devices: /device:TPU:32 before, /device:TPU:1 now
where the time goes in v3:
time: 19.4 us; the launch traced here: 19.2 us
  Pallas kernels  18.4 us (95%)
  local copies, waits for them, and re-layouts  0.75 us (4%)
    pallas_call x1, Pallas kernels, per_device(): pl.pallas_call(lambda *refs: kernel(counts, *refs), out_shape=jax.ShapeDt...  18.4 us
    unnamed x1, local copies, waits for them, and re-layouts  0.75 us

profile of v3, /device:TPU:1, one launch (start us, length us, event | category | flops | bytes accessed | tf_op | source)
XLA Modules:
  0.0 19.2 jit_solution(3636230364818547296)
XLA Ops:
  0.0 18.4 %shard_map.82 = f32[3,256,128]{2,1,0:T(8,128)S(1)} custom-call(f32[3,256,128]{2,1,0:T(8,128)} %bitcast.5, f32[2,96,128]{2,1,0:T(8,128)} %constant.14.clone.refs_1_, bf16[16,256]{1,0:T(8,128)(2,1)} %constant.15.clone.refs_2_, bf16[512,256]{1,0:T(8,128)(2,1)} %constant.16.clone.refs_3_, bf16[256,256]{1,0:T(8,128)(2,1)} %constant.17.clone.refs_4_, ...), custom_call_target="tpu_custom_call" | custom-call | tf_op jit(solution)/shard_map/pallas_call | solution.py:316
  18.4 0.7 %copy.11 = f32[3,256,1,128]{3,2,1,0:T(1,128)} copy(f32[3,256,1,128]{3,2,1,0:T(1,128)S(1)} %bitcast.4) | data formatting | bytes 786432

commit v4 on v3

--- a/solution.py
+++ b/solution.py
@@ -15,6 +15,7 @@
 LZ = 128
 EDGE = 96
 EARLY = 3
+SEAM = 8
 MESH = pl.DeviceIdType.MESH
 
 
@@ -115,8 +116,8 @@
     out,
     v, fade_x, send_z, slope_x, slope_z, spread_z, fade_f, smooth_x,
     fields, part_x, h, h_halves,
-    z_out, z_in, x_out, x_in, f_out, f_in,
-    load_sem, send_sem, recv_sem, ready,
+    z_out, z_in, z_use, z_far, w_far, x_out, x_in, f_out, f_in, ends, extra,
+    load_sem, send_sem, recv_sem, ready, token,
 ):
     nx, nz = counts
     gx, gz = lax.axis_index("gx"), lax.axis_index("gz")
@@ -125,6 +126,10 @@
     sides_z = ((gx, z_next), (gx, z_prev))
     sides_x = ((x_next, gz), (x_prev, gz))
     is_first, is_last = gx == 0, gx == nx - 1
+    ahead, behind = lax.rem(gz, SEAM) == SEAM - 1, lax.rem(gz, SEAM) == 0
+    last_ahead, last_behind = jnp.logical_and(is_last, ahead), jnp.logical_and(is_last, behind)
+    last_seam = jnp.logical_or(last_ahead, last_behind)
+    first_seam = jnp.logical_and(is_first, jnp.logical_or(ahead, behind))
 
     def signal(semaphore, side):
         pl.semaphore_signal(semaphore, inc=1, device_id=side, device_id_type=MESH)
@@ -157,9 +162,19 @@
     for load in loads[:EARLY]:
         load.start()
 
+    z_use[...] = jnp.zeros_like(z_use)
+    z_far[...] = jnp.zeros_like(z_far)
+    extra[...] = jnp.zeros_like(extra)
     barrier = pltpu.get_barrier_semaphore()
-    for side in sides_z + (sides_x[1],):
-        signal(barrier, side)
+    signal(barrier, sides_z[1])
+
+    @pl.when(jnp.logical_not(last_ahead))
+    def _():
+        signal(barrier, sides_z[0])
+
+    @pl.when(jnp.logical_not(is_first))
+    def _():
+        signal(barrier, sides_x[1])
 
     @pl.when(jnp.logical_not(is_last))
     def _():
@@ -191,20 +206,49 @@
             x_out[side, f : f + 1] = scale * total(fade_x[1 - side] * values[f][rows])
             x_out[side, 6 + f : 7 + f] = values[f][row : row + 1]
 
-    pl.semaphore_wait(barrier, jnp.where(is_first, 3, 4))
-    copies = [remote(z_out.at[pl.ds(16 * n, 16)], z_in.at[pl.ds(16 * n, 16)], n, sides_z[n]) for n in (0, 1)]
+    pl.semaphore_wait(barrier, jnp.where(jnp.logical_or(is_first, last_behind), 3, 4))
+
+    @pl.when(last_ahead)
+    def _():
+        signal(token, sides_z[0])
+
+    @pl.when(is_last)
+    def _():
+        signal(ready, sides_x[0])
+
+    @pl.when(is_first)
+    def _():
+        signal(barrier, sides_x[1])
+
+    halves_z = [pl.ds(16 * n, 16) for n in (0, 1)]
+    copies = [remote(z_out.at[halves_z[n]], z_in.at[halves_z[n]], n, sides_z[n]) for n in (0, 1)]
     copies += [remote(x_out.at[n], x_in.at[n], 2 + n, sides_x[n]) for n in (0, 1)]
     copies += [remote(f_out.at[n], f_in.at[n], 4 + n, sides_x[n]) for n in (0, 1)]
-    for n in (0, 1, 2):
-        copies[n].start()
-
-    @pl.when(is_last)
-    def _():
-        signal(ready, sides_x[0])
+    far = [remote(z_out.at[halves_z[n]], z_far.at[halves_z[n]], 6, (x_next, sides_z[n][1])) for n in (0, 1)]
+    far_w = remote(v.at[2], w_far, 7, sides_x[0])
+    copies[0].start()
+
+    @pl.when(jnp.logical_not(last_behind))
+    def _():
+        copies[1].start()
+
+    @pl.when(last_ahead)
+    def _():
+        far[0].start()
+
+    @pl.when(last_behind)
+    def _():
+        far[1].start()
+
+    copies[2].start()
 
     @pl.when(jnp.logical_not(is_first))
     def _():
         copies[3].start()
+
+    @pl.when(last_seam)
+    def _():
+        far_w.start()
 
     loads[3].wait()
     loads[4].wait()
@@ -230,7 +274,7 @@
     f_out[1, 9:10] = total(fade_f[0, top] * (fade_x[0] * v[0, top]))
     f_out[1, 10:11] = v[0, 0:1]
     f_out[1, 11:12] = v[0, 1:2]
-    far = (
+    moments = (
         total(fade_f[1, top] * (fade_x[0] * v[0, top])),
         total(fade_f[0, end] * (fade_x[1] * v[0, end])),
     )
@@ -240,32 +284,65 @@
     far_sum = float(np.sum(rate_f ** (LX - 1 - powers) * rate_d**powers))
     far_end = float(rate_f ** (LX - 1))
 
-    @pl.when(is_first)
-    def _():
-        pl.semaphore_wait(ready, 1)
-        copies[3].start()
-
-    copies[0].wait_recv()
-    copies[1].wait_recv()
-    high, low = split(z_in[...])
-    spread = dot(jnp.concatenate([high, low, high]), spread_z[...], ((0,), (0,)))
-    ends = []
-    for c in range(3):
-        at, to = (3 + c) * 128, c * 128
-        value = h[c] + (spread[:, at : at + 128] + v[2] * spread[:, to : to + 128])
+    def spread_of(sums, w_cells):
+        high, low = split(sums)
+        spread = dot(jnp.concatenate([high, low, high]), spread_z[...], ((0,), (0,)))
+        return [spread[:, n * 128 + 384 : n * 128 + 512] + w_cells * spread[:, n * 128 : n * 128 + 128] for n in range(3)]
+
+    @pl.when(jnp.logical_not(last_behind))
+    def _():
+        copies[0].wait_recv()
+        z_use[0:16] = z_in[0:16]
+
+    @pl.when(jnp.logical_not(last_ahead))
+    def _():
+        copies[1].wait_recv()
+        z_use[16:32] = z_in[16:32]
+
+    for c, part in enumerate(spread_of(z_use[...], v[2])):
+        value = h[c] + part
         h[c] = value
-        ends.append((total(fade_f[1] * value), total(fade_f[0] * value)))
+        ends[0, c : c + 1] = total(fade_f[1] * value)
+        ends[1, c : c + 1] = total(fade_f[0] * value)
 
     first = lax.broadcasted_iota(jnp.int32, (8, LZ), 0) == 0
     last = lax.broadcasted_iota(jnp.int32, (8, LZ), 0) == 7
     for side, (edge, row0, row1) in enumerate(((0, LX - 1, LX - 2), (LX - 1, 0, 1))):
+        if side == 1:
+
+            @pl.when(is_first)
+            def _():
+                pl.semaphore_wait(ready, 1)
+                copies[3].start()
+
+            @pl.when(last_behind)
+            def _():
+                pl.semaphore_wait(token, 1)
+                copies[1].start()
+                copies[0].wait_recv()
+                z_use[0:16] = z_in[0:16]
+                z_use[16:32] = jnp.zeros_like(z_use[16:32])
+
+            @pl.when(last_ahead)
+            def _():
+                copies[1].wait_recv()
+                z_use[16:32] = z_in[16:32]
+                z_use[0:16] = jnp.zeros_like(z_use[0:16])
+
+            @pl.when(last_seam)
+            def _():
+                for c, part in enumerate(spread_of(z_use[...], v[2])):
+                    value = h[c] + part
+                    h[c] = value
+                    ends[1, c : c + 1] = total(fade_f[0] * value)
+
         copies[2 + side].wait_recv()
         sign = near_d if side == 0 else -near_d
         for c in range(3):
             uv, vc = flat[c], 2 + c
-            from_far = far_sum * x_in[side, uv : uv + 1] + far[side] * x_in[side, vc : vc + 1]
+            from_far = far_sum * x_in[side, uv : uv + 1] + moments[side] * x_in[side, vc : vc + 1]
             cell = x_in[side, 6 + uv : 7 + uv] + v[0, edge : edge + 1] * x_in[side, 6 + vc : 7 + vc]
-            f_out[side, c : c + 1] = ends[c][side] + from_far + (sign * far_end) * cell
+            f_out[side, c : c + 1] = ends[side, c : c + 1] + from_far + (sign * far_end) * cell
             f_out[side, 3 + c : 4 + c] = h[c, row0 : row0 + 1]
             f_out[side, 6 + c : 7 + c] = h[c, row1 : row1 + 1]
         copies[4 + side].start()
@@ -285,6 +362,15 @@
         h_halves[c, :, 128:] = low
         full = dot(smooth_x[...], h_halves[c])
         out[c] = full[:LX, :128] + full[:LX, 128:] + full[LX:, :128]
+
+    @pl.when(first_seam)
+    def _():
+        far[0].wait_recv()
+        far_w.wait_recv()
+        for c, part in enumerate(spread_of(z_far[...], w_far[...])):
+            extra[c : c + 1] = total(fade_f[1] * part)
+            extra[3 + c : 4 + c] = part[LX - 1 : LX]
+            extra[6 + c : 7 + c] = part[LX - 2 : LX - 1]
 
     row = lax.broadcasted_iota(jnp.int32, (8, LZ), 0)
     copies[5].wait_recv()
@@ -297,16 +383,22 @@
             own, own_v = x_out[1 - side, uv : uv + 1], x_out[1 - side, vc : vc + 1]
             edge, edge_v = x_out[1 - side, 6 + uv : 7 + uv], x_out[1 - side, 6 + vc : 7 + vc]
             moment, u1, u2 = (f_in[side, n : n + 1] for n in (9, 10, 11))
+            sent = [f_in[side, n : n + 1] + (extra[n : n + 1] if side == 0 else 0.0) for n in (c, 3 + c, 6 + c)]
             cell = sign * (edge + u1 * edge_v)
-            sums.append(scale * (f_in[side, c : c + 1] + near_sum * own + moment * own_v + cell))
-            cell1 = f_in[side, 3 + c : 4 + c] + own + u1 * own_v + cell
-            cell2 = f_in[side, 6 + c : 7 + c] + rate_d * (own + u2 * own_v)
+            sums.append(scale * (sent[0] + near_sum * own + moment * own_v + cell))
+            cell1 = sent[1] + own + u1 * own_v + cell
+            cell2 = sent[2] + rate_d * (own + u2 * own_v)
             out[c, start : start + 8] += jnp.where(row == end0, near1 * cell1 + near2 * cell2, 0.0) + jnp.where(
                 row == end1, near2 * cell1, 0.0
             )
         out[c] += fade_f[0] * sums[0] + fade_f[1] * sums[1]
     for copy in copies:
         copy.wait_send()
+
+    @pl.when(last_seam)
+    def _():
+        far[0].wait_send()
+        far_w.wait_send()
 
 
 def per_device(counts, velocity):
@@ -327,13 +419,19 @@
             pltpu.VMEM((3, LX, 2 * LZ), bf16),
             pltpu.VMEM((32, LX), f32),
             pltpu.VMEM((32, LX), f32),
+            pltpu.VMEM((32, LX), f32),
+            pltpu.VMEM((32, LX), f32),
+            pltpu.VMEM((LX, LZ), f32),
             pltpu.VMEM((2, 16, LZ), f32),
             pltpu.VMEM((2, 16, LZ), f32),
             pltpu.VMEM((2, 16, LZ), f32),
             pltpu.VMEM((2, 16, LZ), f32),
+            pltpu.VMEM((2, 8, LZ), f32),
+            pltpu.VMEM((16, LZ), f32),
             pltpu.SemaphoreType.DMA((8,)),
-            pltpu.SemaphoreType.DMA((6,)),
-            pltpu.SemaphoreType.DMA((6,)),
+            pltpu.SemaphoreType.DMA((8,)),
+            pltpu.SemaphoreType.DMA((8,)),
+            pltpu.SemaphoreType.REGULAR,
             pltpu.SemaphoreType.REGULAR,
         ],
         compiler_params=pltpu.CompilerParams(collective_id=0, has_side_effects=True, vmem_limit_bytes=32 * 2**20),

time: 19.4 us -> 18.4 us (0.948)
  Pallas kernels: 18.4 us -> 17.5 us
    pallas_call x1, Pallas kernels: 18.4 us -> 17.5 us  [per_device(): pl.pallas_call(lambda *refs: kernel(counts, *refs), out_shape=jax.ShapeDt...]
where the time goes in v4:
time: 18.4 us; the launch traced here: 18.3 us
  Pallas kernels  17.5 us (95%)
  local copies, waits for them, and re-layouts  0.75 us (4%)
    pallas_call x1, Pallas kernels, per_device(): pl.pallas_call(lambda *refs: kernel(counts, *refs), out_shape=jax.ShapeDt...  17.5 us
    unnamed x1, local copies, waits for them, and re-layouts  0.75 us

profile of v4, /device:TPU:1, one launch (start us, length us, event | category | flops | bytes accessed | tf_op | source)
XLA Modules:
  0.0 18.3 jit_solution(13533120385209524030)
XLA Ops:
  0.0 17.5 %shard_map.82 = f32[3,256,128]{2,1,0:T(8,128)S(1)} custom-call(f32[3,256,128]{2,1,0:T(8,128)} %bitcast.5, f32[2,96,128]{2,1,0:T(8,128)} %constant.14.clone.refs_1_, bf16[16,256]{1,0:T(8,128)(2,1)} %constant.15.clone.refs_2_, bf16[512,256]{1,0:T(8,128)(2,1)} %constant.16.clone.refs_3_, bf16[256,256]{1,0:T(8,128)(2,1)} %constant.17.clone.refs_4_, ...), custom_call_target="tpu_custom_call" | custom-call | tf_op jit(solution)/shard_map/pallas_call | solution.py:408
  17.5 0.7 %copy.11 = f32[3,256,1,128]{3,2,1,0:T(1,128)} copy(f32[3,256,1,128]{3,2,1,0:T(1,128)S(1)} %bitcast.4) | data formatting | bytes 786432

commit v5 on v4

--- a/solution.py
+++ b/solution.py
@@ -116,7 +116,7 @@
     out,
     v, fade_x, send_z, slope_x, slope_z, spread_z, fade_f, smooth_x,
     fields, part_x, h, h_halves,
-    z_out, z_in, z_use, z_far, w_far, x_out, x_in, f_out, f_in, ends, extra,
+    z_out, z_in, z_use, z_far, w_far, x_out, x_in, x_use, x_far, f_out, f_in, ends, extra,
     load_sem, send_sem, recv_sem, ready, token,
 ):
     nx, nz = counts
@@ -126,7 +126,9 @@
     sides_z = ((gx, z_next), (gx, z_prev))
     sides_x = ((x_next, gz), (x_prev, gz))
     is_first, is_last = gx == 0, gx == nx - 1
-    ahead, behind = lax.rem(gz, SEAM) == SEAM - 1, lax.rem(gz, SEAM) == 0
+    ahead = jnp.logical_or(lax.rem(gz, SEAM) == SEAM - 1, gz == 1)
+    behind = jnp.logical_or(lax.rem(gz, SEAM) == 0, gz == 2)
+    is_second_last = gx == nx - 2
     last_ahead, last_behind = jnp.logical_and(is_last, ahead), jnp.logical_and(is_last, behind)
     last_seam = jnp.logical_or(last_ahead, last_behind)
     first_seam = jnp.logical_and(is_first, jnp.logical_or(ahead, behind))
@@ -164,6 +166,8 @@
 
     z_use[...] = jnp.zeros_like(z_use)
     z_far[...] = jnp.zeros_like(z_far)
+    x_use[...] = jnp.zeros_like(x_use)
+    x_far[...] = jnp.zeros_like(x_far)
     extra[...] = jnp.zeros_like(extra)
     barrier = pltpu.get_barrier_semaphore()
     signal(barrier, sides_z[1])
@@ -206,7 +210,8 @@
             x_out[side, f : f + 1] = scale * total(fade_x[1 - side] * values[f][rows])
             x_out[side, 6 + f : 7 + f] = values[f][row : row + 1]
 
-    pl.semaphore_wait(barrier, jnp.where(jnp.logical_or(is_first, last_behind), 3, 4))
+    fewer = jnp.where(jnp.logical_or(is_first, last_behind), 1, 0)
+    pl.semaphore_wait(barrier, 4 - fewer + jnp.where(is_second_last, 1, 0))
 
     @pl.when(last_ahead)
     def _():
@@ -219,6 +224,7 @@
     @pl.when(is_first)
     def _():
         signal(barrier, sides_x[1])
+        signal(barrier, (nx - 2, gz))
 
     halves_z = [pl.ds(16 * n, 16) for n in (0, 1)]
     copies = [remote(z_out.at[halves_z[n]], z_in.at[halves_z[n]], n, sides_z[n]) for n in (0, 1)]
@@ -226,6 +232,7 @@
     copies += [remote(f_out.at[n], f_in.at[n], 4 + n, sides_x[n]) for n in (0, 1)]
     far = [remote(z_out.at[halves_z[n]], z_far.at[halves_z[n]], 6, (x_next, sides_z[n][1])) for n in (0, 1)]
     far_w = remote(v.at[2], w_far, 7, sides_x[0])
+    far_x = remote(x_out.at[0], x_far, 8, (0, gz))
     copies[0].start()
 
     @pl.when(jnp.logical_not(last_behind))
@@ -242,11 +249,15 @@
 
     copies[2].start()
 
+    @pl.when(is_second_last)
+    def _():
+        far_x.start()
+
     @pl.when(jnp.logical_not(is_first))
     def _():
         copies[3].start()
 
-    @pl.when(last_seam)
+    @pl.when(jnp.logical_and(last_seam, gz != 0))
     def _():
         far_w.start()
 
@@ -274,10 +285,12 @@
     f_out[1, 9:10] = total(fade_f[0, top] * (fade_x[0] * v[0, top]))
     f_out[1, 10:11] = v[0, 0:1]
     f_out[1, 11:12] = v[0, 1:2]
+    f_out[0, 13:14] = v[0, 0:1]
     moments = (
         total(fade_f[1, top] * (fade_x[0] * v[0, top])),
         total(fade_f[0, end] * (fade_x[1] * v[0, end])),
     )
+    f_out[0, 12:13] = moments[0]
     rate_f, factor_f, (near1, near2) = smooth_kernel()[1:]
     powers = np.arange(EDGE, dtype=np.float64)
     near_sum = float(np.sum((rate_f * rate_d) ** powers))
@@ -288,6 +301,10 @@
         high, low = split(sums)
         spread = dot(jnp.concatenate([high, low, high]), spread_z[...], ((0,), (0,)))
         return [spread[:, n * 128 + 384 : n * 128 + 512] + w_cells * spread[:, n * 128 : n * 128 + 128] for n in range(3)]
+
+    @pl.when(jnp.logical_and(last_seam, gz == 0))
+    def _():
+        far_w.start()
 
     @pl.when(jnp.logical_not(last_behind))
     def _():
@@ -336,16 +353,28 @@
                     h[c] = value
                     ends[1, c : c + 1] = total(fade_f[0] * value)
 
-        copies[2 + side].wait_recv()
+            copies[3].wait_recv()
+            x_use[1] = x_in[1]
+        else:
+
+            @pl.when(jnp.logical_not(is_last))
+            def _():
+                copies[2].wait_recv()
+                x_use[0] = x_in[0]
+
         sign = near_d if side == 0 else -near_d
         for c in range(3):
             uv, vc = flat[c], 2 + c
-            from_far = far_sum * x_in[side, uv : uv + 1] + moments[side] * x_in[side, vc : vc + 1]
-            cell = x_in[side, 6 + uv : 7 + uv] + v[0, edge : edge + 1] * x_in[side, 6 + vc : 7 + vc]
+            from_far = far_sum * x_use[side, uv : uv + 1] + moments[side] * x_use[side, vc : vc + 1]
+            cell = x_use[side, 6 + uv : 7 + uv] + v[0, edge : edge + 1] * x_use[side, 6 + vc : 7 + vc]
             f_out[side, c : c + 1] = ends[side, c : c + 1] + from_far + (sign * far_end) * cell
             f_out[side, 3 + c : 4 + c] = h[c, row0 : row0 + 1]
             f_out[side, 6 + c : 7 + c] = h[c, row1 : row1 + 1]
         copies[4 + side].start()
+
+    @pl.when(is_last)
+    def _():
+        copies[2].wait_recv()
 
     for c in range(3):
         uv, vc = flat[c], 2 + c
@@ -362,6 +391,10 @@
         h_halves[c, :, 128:] = low
         full = dot(smooth_x[...], h_halves[c])
         out[c] = full[:LX, :128] + full[:LX, 128:] + full[LX:, :128]
+
+    @pl.when(is_first)
+    def _():
+        far_x.wait_recv()
 
     @pl.when(first_seam)
     def _():
@@ -385,6 +418,10 @@
             moment, u1, u2 = (f_in[side, n : n + 1] for n in (9, 10, 11))
             sent = [f_in[side, n : n + 1] + (extra[n : n + 1] if side == 0 else 0.0) for n in (c, 3 + c, 6 + c)]
             cell = sign * (edge + u1 * edge_v)
+            if side == 0:
+                cell_far = x_far[6 + uv : 7 + uv] + f_in[0, 13:14] * x_far[6 + vc : 7 + vc]
+                from_far = far_sum * x_far[uv : uv + 1] + f_in[0, 12:13] * x_far[vc : vc + 1]
+                sent[0] += from_far + (near_d * far_end) * cell_far
             sums.append(scale * (sent[0] + near_sum * own + moment * own_v + cell))
             cell1 = sent[1] + own + u1 * own_v + cell
             cell2 = sent[2] + rate_d * (own + u2 * own_v)
@@ -394,6 +431,10 @@
         out[c] += fade_f[0] * sums[0] + fade_f[1] * sums[1]
     for copy in copies:
         copy.wait_send()
+
+    @pl.when(is_second_last)
+    def _():
+        far_x.wait_send()
 
     @pl.when(last_seam)
     def _():
@@ -425,12 +466,14 @@
             pltpu.VMEM((2, 16, LZ), f32),
             pltpu.VMEM((2, 16, LZ), f32),
             pltpu.VMEM((2, 16, LZ), f32),
+            pltpu.VMEM((16, LZ), f32),
+            pltpu.VMEM((2, 16, LZ), f32),
             pltpu.VMEM((2, 16, LZ), f32),
             pltpu.VMEM((2, 8, LZ), f32),
             pltpu.VMEM((16, LZ), f32),
             pltpu.SemaphoreType.DMA((8,)),
-            pltpu.SemaphoreType.DMA((8,)),
-            pltpu.SemaphoreType.DMA((8,)),
+            pltpu.SemaphoreType.DMA((9,)),
+            pltpu.SemaphoreType.DMA((9,)),
             pltpu.SemaphoreType.REGULAR,
             pltpu.SemaphoreType.REGULAR,
         ],

time: 18.4 us -> 17.6 us (0.957)
  Pallas kernels: 17.5 us -> 16.7 us
    pallas_call x1, Pallas kernels: 17.5 us -> 16.7 us  [per_device(): pl.pallas_call(lambda *refs: kernel(counts, *refs), out_shape=jax.ShapeDt...]
where the time goes in v5:
time: 17.6 us; the launch traced here: 17.5 us
  Pallas kernels  16.7 us (95%)
  local copies, waits for them, and re-layouts  0.75 us (4%)
    pallas_call x1, Pallas kernels, per_device(): pl.pallas_call(lambda *refs: kernel(counts, *refs), out_shape=jax.ShapeDt...  16.7 us
    unnamed x1, local copies, waits for them, and re-layouts  0.75 us

profile of v5, /device:TPU:1, one launch (start us, length us, event | category | flops | bytes accessed | tf_op | source)
XLA Modules:
  0.0 17.5 jit_solution(1351881553036409882)
XLA Ops:
  0.0 16.7 %shard_map.82 = f32[3,256,128]{2,1,0:T(8,128)S(1)} custom-call(f32[3,256,128]{2,1,0:T(8,128)} %bitcast.5, f32[2,96,128]{2,1,0:T(8,128)} %constant.14.clone.refs_1_, bf16[16,256]{1,0:T(8,128)(2,1)} %constant.15.clone.refs_2_, bf16[512,256]{1,0:T(8,128)(2,1)} %constant.16.clone.refs_3_, bf16[256,256]{1,0:T(8,128)(2,1)} %constant.17.clone.refs_4_, ...), custom_call_target="tpu_custom_call" | custom-call | tf_op jit(solution)/shard_map/pallas_call | solution.py:449
  16.7 0.7 %copy.11 = f32[3,256,1,128]{3,2,1,0:T(1,128)} copy(f32[3,256,1,128]{3,2,1,0:T(1,128)S(1)} %bitcast.4) | data formatting | bytes 786432

commit v6 on v5

--- a/solution.py
+++ b/solution.py
@@ -83,6 +83,7 @@
         spread[2 * f + 1, f, 0] = near
         spread[16 + 2 * f, f] = rate ** (LZ - 1.0 - k)
         spread[17 + 2 * f, f, LZ - 1] = -near
+    basis = np.stack([spread[:, :3].sum(axis=1), spread[:, 3:].sum(axis=1)]).astype(np.float32)
     high, low = halves(spread.reshape(32, 6 * LZ))
     spread_z = np.concatenate([high, high, low])
     fade_x = np.zeros((2, EDGE, LZ), np.float32)
@@ -93,7 +94,7 @@
     fade_f = np.zeros((2, LX, LZ), np.float32)
     fade_f[0] = (rate**i)[:, None]
     fade_f[1] = fade_f[0, ::-1]
-    return fade_x, send_z, slope_x, slope_z, spread_z, fade_f, smooth_x
+    return fade_x, send_z, slope_x, slope_z, spread_z, fade_f, smooth_x, basis
 
 
 def split(values):
@@ -112,10 +113,10 @@
 
 def kernel(
     counts,
-    velocity_hbm, fade_x_hbm, send_z_hbm, slope_x_hbm, slope_z_hbm, spread_z_hbm, fade_f_hbm, smooth_x_hbm,
+    velocity_hbm, fade_x_hbm, send_z_hbm, slope_x_hbm, slope_z_hbm, spread_z_hbm, fade_f_hbm, smooth_x_hbm, basis_hbm,
     out,
-    v, fade_x, send_z, slope_x, slope_z, spread_z, fade_f, smooth_x,
-    fields, part_x, h, h_halves,
+    v, fade_x, send_z, slope_x, slope_z, spread_z, fade_f, smooth_x, basis,
+    fields, weights, part_x, h, h_halves,
     z_out, z_in, z_use, z_far, w_far, x_out, x_in, x_use, x_far, f_out, f_in, ends, extra,
     load_sem, send_sem, recv_sem, ready, token,
 ):
@@ -158,6 +159,7 @@
                 (spread_z_hbm, spread_z),
                 (fade_f_hbm, fade_f),
                 (smooth_x_hbm, smooth_x),
+                (basis_hbm, basis),
             )
         )
     ]
@@ -202,6 +204,43 @@
         z_out[2 * f : 2 * f + 2] = both[0:2]
         z_out[16 + 2 * f : 18 + 2 * f] = both[2:4]
 
+    fewer = jnp.where(jnp.logical_or(is_first, last_behind), 1, 0)
+    pl.semaphore_wait(barrier, 4 - fewer + jnp.where(is_second_last, 1, 0))
+
+    @pl.when(last_ahead)
+    def _():
+        signal(token, sides_z[0])
+
+    @pl.when(is_last)
+    def _():
+        signal(ready, sides_x[0])
+
+    @pl.when(is_first)
+    def _():
+        signal(barrier, sides_x[1])
+        signal(barrier, (nx - 2, gz))
+
+    halves_z = [pl.ds(16 * n, 16) for n in (0, 1)]
+    copies = [remote(z_out.at[halves_z[n]], z_in.at[halves_z[n]], n, sides_z[n]) for n in (0, 1)]
+    copies += [remote(x_out.at[n], x_in.at[n], 2 + n, sides_x[n]) for n in (0, 1)]
+    copies += [remote(f_out.at[n], f_in.at[n], 4 + n, sides_x[n]) for n in (0, 1)]
+    far = [remote(z_out.at[halves_z[n]], z_far.at[halves_z[n]], 6, (x_next, sides_z[n][1])) for n in (0, 1)]
+    far_w = remote(v.at[2], w_far, 7, sides_x[0])
+    far_x = remote(x_out.at[0], x_far, 8, (0, gz))
+    @pl.when(last_ahead)
+    def _():
+        far[0].start()
+
+    @pl.when(last_behind)
+    def _():
+        far[1].start()
+
+    @pl.when(jnp.logical_not(last_behind))
+    def _():
+        copies[1].start()
+
+    copies[0].start()
+
     rate_d, factor_d, near_d = slope_kernel()[1:]
     for side, row in ((0, LX - 1), (1, 0)):
         rows = slice(LX - EDGE, LX) if side == 0 else slice(0, EDGE)
@@ -209,43 +248,6 @@
         for f in range(6):
             x_out[side, f : f + 1] = scale * total(fade_x[1 - side] * values[f][rows])
             x_out[side, 6 + f : 7 + f] = values[f][row : row + 1]
-
-    fewer = jnp.where(jnp.logical_or(is_first, last_behind), 1, 0)
-    pl.semaphore_wait(barrier, 4 - fewer + jnp.where(is_second_last, 1, 0))
-
-    @pl.when(last_ahead)
-    def _():
-        signal(token, sides_z[0])
-
-    @pl.when(is_last)
-    def _():
-        signal(ready, sides_x[0])
-
-    @pl.when(is_first)
-    def _():
-        signal(barrier, sides_x[1])
-        signal(barrier, (nx - 2, gz))
-
-    halves_z = [pl.ds(16 * n, 16) for n in (0, 1)]
-    copies = [remote(z_out.at[halves_z[n]], z_in.at[halves_z[n]], n, sides_z[n]) for n in (0, 1)]
-    copies += [remote(x_out.at[n], x_in.at[n], 2 + n, sides_x[n]) for n in (0, 1)]
-    copies += [remote(f_out.at[n], f_in.at[n], 4 + n, sides_x[n]) for n in (0, 1)]
-    far = [remote(z_out.at[halves_z[n]], z_far.at[halves_z[n]], 6, (x_next, sides_z[n][1])) for n in (0, 1)]
-    far_w = remote(v.at[2], w_far, 7, sides_x[0])
-    far_x = remote(x_out.at[0], x_far, 8, (0, gz))
-    copies[0].start()
-
-    @pl.when(jnp.logical_not(last_behind))
-    def _():
-        copies[1].start()
-
-    @pl.when(last_ahead)
-    def _():
-        far[0].start()
-
-    @pl.when(last_behind)
-    def _():
-        far[1].start()
 
     copies[2].start()
 
@@ -302,6 +304,33 @@
         spread = dot(jnp.concatenate([high, low, high]), spread_z[...], ((0,), (0,)))
         return [spread[:, n * 128 + 384 : n * 128 + 512] + w_cells * spread[:, n * 128 : n * 128 + 128] for n in range(3)]
 
+    def weigh(w_cells):
+        high, low = split(fade_f[1] * w_cells)
+        weights[:, :128] = high
+        weights[:, 128:256] = low
+
+    def message_of(sums, w_end):
+        high, low = split(sums)
+        full = dot(jnp.concatenate([high, low]), weights[...])
+        by_w = full[:32, :128] + full[:32, 128:256] + full[32:, :128]
+        plain = full[:32, 256:384] + full[:32, 384:] + full[32:, 256:384]
+        terms = [basis[0] * by_w + basis[1] * plain]
+        for n in (1, 2):
+            cell = jnp.broadcast_to(sums[:, LX - n : LX - n + 1], (32, LZ))
+            terms.append(cell * (basis[0] * w_end[8 - n : 9 - n] + basis[1]))
+        both = [term[:16] + term[16:] for term in terms]
+        return [
+            [t[2 * c : 2 * c + 1] + t[2 * c + 1 : 2 * c + 2] + t[6 + 2 * c : 7 + 2 * c] + t[7 + 2 * c : 8 + 2 * c] for t in both]
+            for c in range(3)
+        ]
+
+    high, low = split(fade_f[1])
+    weights[:, 256:384] = high
+    weights[:, 384:] = low
+    weigh(v[2])
+    for c in range(3):
+        ends[0, c : c + 1] = total(fade_f[1] * h[c])
+
     @pl.when(jnp.logical_and(last_seam, gz == 0))
     def _():
         far_w.start()
@@ -316,61 +345,59 @@
         copies[1].wait_recv()
         z_use[16:32] = z_in[16:32]
 
-    for c, part in enumerate(spread_of(z_use[...], v[2])):
-        value = h[c] + part
-        h[c] = value
-        ends[0, c : c + 1] = total(fade_f[1] * value)
-        ends[1, c : c + 1] = total(fade_f[0] * value)
+    @pl.when(jnp.logical_not(is_last))
+    def _():
+        copies[2].wait_recv()
+        x_use[0] = x_in[0]
 
     first = lax.broadcasted_iota(jnp.int32, (8, LZ), 0) == 0
     last = lax.broadcasted_iota(jnp.int32, (8, LZ), 0) == 7
-    for side, (edge, row0, row1) in enumerate(((0, LX - 1, LX - 2), (LX - 1, 0, 1))):
-        if side == 1:
-
-            @pl.when(is_first)
-            def _():
-                pl.semaphore_wait(ready, 1)
-                copies[3].start()
-
-            @pl.when(last_behind)
-            def _():
-                pl.semaphore_wait(token, 1)
-                copies[1].start()
-                copies[0].wait_recv()
-                z_use[0:16] = z_in[0:16]
-                z_use[16:32] = jnp.zeros_like(z_use[16:32])
-
-            @pl.when(last_ahead)
-            def _():
-                copies[1].wait_recv()
-                z_use[16:32] = z_in[16:32]
-                z_use[0:16] = jnp.zeros_like(z_use[0:16])
-
-            @pl.when(last_seam)
-            def _():
-                for c, part in enumerate(spread_of(z_use[...], v[2])):
-                    value = h[c] + part
-                    h[c] = value
-                    ends[1, c : c + 1] = total(fade_f[0] * value)
-
-            copies[3].wait_recv()
-            x_use[1] = x_in[1]
-        else:
-
-            @pl.when(jnp.logical_not(is_last))
-            def _():
-                copies[2].wait_recv()
-                x_use[0] = x_in[0]
-
-        sign = near_d if side == 0 else -near_d
-        for c in range(3):
-            uv, vc = flat[c], 2 + c
-            from_far = far_sum * x_use[side, uv : uv + 1] + moments[side] * x_use[side, vc : vc + 1]
-            cell = x_use[side, 6 + uv : 7 + uv] + v[0, edge : edge + 1] * x_use[side, 6 + vc : 7 + vc]
-            f_out[side, c : c + 1] = ends[side, c : c + 1] + from_far + (sign * far_end) * cell
-            f_out[side, 3 + c : 4 + c] = h[c, row0 : row0 + 1]
-            f_out[side, 6 + c : 7 + c] = h[c, row1 : row1 + 1]
-        copies[4 + side].start()
+
+    def write_message(side, c, value, cell1, cell2):
+        uv, vc = flat[c], 2 + c
+        edge, sign = (0, near_d) if side == 0 else (LX - 1, -near_d)
+        from_far = far_sum * x_use[side, uv : uv + 1] + moments[side] * x_use[side, vc : vc + 1]
+        cell = x_use[side, 6 + uv : 7 + uv] + v[0, edge : edge + 1] * x_use[side, 6 + vc : 7 + vc]
+        f_out[side, c : c + 1] = value + from_far + (sign * far_end) * cell
+        f_out[side, 3 + c : 4 + c] = cell1
+        f_out[side, 6 + c : 7 + c] = cell2
+
+    for c, (value, cell1, cell2) in enumerate(message_of(z_use[...], v[2, LX - 8 : LX])):
+        write_message(0, c, ends[0, c : c + 1] + value, h[c, LX - 1 : LX] + cell1, h[c, LX - 2 : LX - 1] + cell2)
+    copies[4].start()
+
+    for c, part in enumerate(spread_of(z_use[...], v[2])):
+        h[c] += part
+
+    @pl.when(is_first)
+    def _():
+        pl.semaphore_wait(ready, 1)
+        copies[3].start()
+
+    @pl.when(last_behind)
+    def _():
+        pl.semaphore_wait(token, 1)
+        copies[1].start()
+        copies[0].wait_recv()
+        z_use[0:16] = z_in[0:16]
+        z_use[16:32] = jnp.zeros_like(z_use[16:32])
+
+    @pl.when(last_ahead)
+    def _():
+        copies[1].wait_recv()
+        z_use[16:32] = z_in[16:32]
+        z_use[0:16] = jnp.zeros_like(z_use[0:16])
+
+    @pl.when(last_seam)
+    def _():
+        for c, part in enumerate(spread_of(z_use[...], v[2])):
+            h[c] += part
+
+    copies[3].wait_recv()
+    x_use[1] = x_in[1]
+    for c in range(3):
+        write_message(1, c, total(fade_f[0] * h[c]), h[c, 0:1], h[c, 1:2])
+    copies[5].start()
 
     @pl.when(is_last)
     def _():
@@ -398,12 +425,12 @@
 
     @pl.when(first_seam)
     def _():
+        far_w.wait_recv()
+        weigh(w_far[...])
         far[0].wait_recv()
-        far_w.wait_recv()
-        for c, part in enumerate(spread_of(z_far[...], w_far[...])):
-            extra[c : c + 1] = total(fade_f[1] * part)
-            extra[3 + c : 4 + c] = part[LX - 1 : LX]
-            extra[6 + c : 7 + c] = part[LX - 2 : LX - 1]
+        for c, parts in enumerate(message_of(z_far[...], w_far[LX - 8 : LX])):
+            for n, part in enumerate(parts):
+                extra[3 * n + c : 3 * n + c + 1] = part
 
     row = lax.broadcasted_iota(jnp.int32, (8, LZ), 0)
     copies[5].wait_recv()
@@ -449,12 +476,13 @@
     out = pl.pallas_call(
         lambda *refs: kernel(counts, *refs),
         out_shape=jax.ShapeDtypeStruct((3, LX, LZ), f32),
-        in_specs=[pl.BlockSpec(memory_space=pltpu.HBM)] * 8,
+        in_specs=[pl.BlockSpec(memory_space=pltpu.HBM)] * 9,
         out_specs=pl.BlockSpec(memory_space=pltpu.VMEM),
         scratch_shapes=[pltpu.VMEM((3, LX, LZ), f32)]
         + [pltpu.VMEM(t.shape, t.dtype) for t in operands]
         + [
             pltpu.VMEM((LX, 8 * 256), bf16),
+            pltpu.VMEM((LX, 4 * LZ), bf16),
             pltpu.VMEM((6, LX, LZ), f32),
             pltpu.VMEM((3, LX, LZ), f32),
             pltpu.VMEM((3, LX, 2 * LZ), bf16),
@@ -469,9 +497,9 @@
             pltpu.VMEM((16, LZ), f32),
             pltpu.VMEM((2, 16, LZ), f32),
             pltpu.VMEM((2, 16, LZ), f32),
-            pltpu.VMEM((2, 8, LZ), f32),
+            pltpu.VMEM((1, 8, LZ), f32),
             pltpu.VMEM((16, LZ), f32),
-            pltpu.SemaphoreType.DMA((8,)),
+            pltpu.SemaphoreType.DMA((9,)),
             pltpu.SemaphoreType.DMA((9,)),
             pltpu.SemaphoreType.DMA((9,)),
             pltpu.SemaphoreType.REGULAR,

time: 17.6 us -> 17.5 us (level)
  Pallas kernels: 16.7 us -> 16.5 us
where the time goes in v6:
time: 17.5 us; the launch traced here: 17.3 us
  Pallas kernels  16.5 us (94%)
  local copies, waits for them, and re-layouts  0.75 us (4%)
    pallas_call x1, Pallas kernels, per_device(): pl.pallas_call(lambda *refs: kernel(counts, *refs), out_shape=jax.ShapeDt...  16.5 us
    unnamed x1, local copies, waits for them, and re-layouts  0.75 us

profile of v6, /device:TPU:1, one launch (start us, length us, event | category | flops | bytes accessed | tf_op | source)
XLA Modules:
  0.0 17.3 jit_solution(1731160474485656647)
XLA Ops:
  0.0 16.5 %shard_map.91 = f32[3,256,128]{2,1,0:T(8,128)S(1)} custom-call(f32[3,256,128]{2,1,0:T(8,128)} %bitcast.5, f32[2,96,128]{2,1,0:T(8,128)} %constant.16.clone.refs_1_, bf16[16,256]{1,0:T(8,128)(2,1)} %constant.17.clone.refs_2_, bf16[512,256]{1,0:T(8,128)(2,1)} %constant.18.clone.refs_3_, bf16[256,256]{1,0:T(8,128)(2,1)} %constant.19.clone.refs_4_, ...), custom_call_target="tpu_custom_call" | custom-call | tf_op jit(solution)/shard_map/pallas_call | solution.py:476
  16.6 0.7 %copy.12 = f32[3,256,1,128]{3,2,1,0:T(1,128)} copy(f32[3,256,1,128]{3,2,1,0:T(1,128)S(1)} %bitcast.4) | data formatting | bytes 786432

commit v7 on v6

--- a/solution.py
+++ b/solution.py
@@ -14,7 +14,7 @@
 LX = 256
 LZ = 128
 EDGE = 96
-EARLY = 3
+PIECE = 256
 SEAM = 8
 MESH = pl.DeviceIdType.MESH
 
@@ -151,7 +151,6 @@
         pltpu.make_async_copy(src, dst, load_sem.at[n])
         for n, (src, dst) in enumerate(
             (
-                (velocity_hbm, v),
                 (fade_x_hbm, fade_x),
                 (send_z_hbm, send_z),
                 (slope_x_hbm, slope_x),
@@ -163,14 +162,20 @@
             )
         )
     ]
-    for load in loads[:EARLY]:
+    pieces = [
+        pltpu.make_async_copy(
+            velocity_hbm.at[c, pl.ds(r * PIECE, PIECE)],
+            v.at[c, pl.ds(r * PIECE, PIECE)],
+            load_sem.at[len(loads) + c * (LX // PIECE) + r],
+        )
+        for c in range(3)
+        for r in range(LX // PIECE)
+    ]
+    for load in pieces + loads[:2]:
         load.start()
 
-    z_use[...] = jnp.zeros_like(z_use)
     z_far[...] = jnp.zeros_like(z_far)
-    x_use[...] = jnp.zeros_like(x_use)
     x_far[...] = jnp.zeros_like(x_far)
-    extra[...] = jnp.zeros_like(extra)
     barrier = pltpu.get_barrier_semaphore()
     signal(barrier, sides_z[1])
 
@@ -186,17 +191,22 @@
     def _():
         signal(barrier, sides_x[0])
 
-    z_out[...] = jnp.zeros_like(z_out)
-    for load in loads[:3]:
+    for ref in (z_out, z_use, x_use, extra):
+        ref[...] = jnp.zeros_like(ref)
+    for load in pieces + loads[1:2]:
         load.wait()
-    for load in loads[EARLY:]:
+    for load in loads[2:]:
         load.start()
     u, w = v[0], v[2]
     values = (u * u, u * v[1], u, v[1], w, u * w, w * v[1], w * w)
-    for n in (2, 3, 4, 5, 6, 7, 0, 1):
+
+    def store_field(n):
         high, low = split(values[n])
         fields[:, n * 256 : n * 256 + 128] = high
         fields[:, n * 256 + 128 : n * 256 + 256] = low
+
+    for n in range(2, 8):
+        store_field(n)
 
     for f in range(6):
         both = dot(send_z[...], fields[:, (2 + f) * 256 : (3 + f) * 256], ((1,), (1,)))
@@ -241,6 +251,7 @@
 
     copies[0].start()
 
+    loads[0].wait()
     rate_d, factor_d, near_d = slope_kernel()[1:]
     for side, row in ((0, LX - 1), (1, 0)):
         rows = slice(LX - EDGE, LX) if side == 0 else slice(0, EDGE)
@@ -263,8 +274,10 @@
     def _():
         far_w.start()
 
+    for n in (0, 1):
+        store_field(n)
+    loads[2].wait()
     loads[3].wait()
-    loads[4].wait()
     flat = (0, 1, 5)
     for f in range(6):
         full = dot(slope_x[...], fields[:, f * 256 : f * 256 + 256])
@@ -277,7 +290,7 @@
             value = value + (v[2] * part if by_w else part)
         h[c] = value
 
-    for load in loads[5:]:
+    for load in loads[4:]:
         load.wait()
 
     top, end = slice(0, EDGE), slice(LX - EDGE, LX)
@@ -499,7 +512,7 @@
             pltpu.VMEM((2, 16, LZ), f32),
             pltpu.VMEM((1, 8, LZ), f32),
             pltpu.VMEM((16, LZ), f32),
-            pltpu.SemaphoreType.DMA((9,)),
+            pltpu.SemaphoreType.DMA((8 + 3 * LX // PIECE,)),
             pltpu.SemaphoreType.DMA((9,)),
             pltpu.SemaphoreType.DMA((9,)),
             pltpu.SemaphoreType.REGULAR,

time: 17.5 us -> 17.4 us (level)
  no operation moved by 1% of the time
where the time goes in v7:
time: 17.4 us; the launch traced here: 17.3 us
  Pallas kernels  16.5 us (95%)
  local copies, waits for them, and re-layouts  0.75 us (4%)
    pallas_call x1, Pallas kernels, per_device(): pl.pallas_call(lambda *refs: kernel(counts, *refs), out_shape=jax.ShapeDt...  16.5 us
    unnamed x1, local copies, waits for them, and re-layouts  0.75 us

profile of v7, /device:TPU:1, one launch (start us, length us, event | category | flops | bytes accessed | tf_op | source)
XLA Modules:
  0.0 17.3 jit_solution(3822074797176541294)
XLA Ops:
  0.0 16.5 %shard_map.91 = f32[3,256,128]{2,1,0:T(8,128)S(1)} custom-call(f32[3,256,128]{2,1,0:T(8,128)} %bitcast.5, f32[2,96,128]{2,1,0:T(8,128)} %constant.16.clone.refs_1_, bf16[16,256]{1,0:T(8,128)(2,1)} %constant.17.clone.refs_2_, bf16[512,256]{1,0:T(8,128)(2,1)} %constant.18.clone.refs_3_, bf16[256,256]{1,0:T(8,128)(2,1)} %constant.19.clone.refs_4_, ...), custom_call_target="tpu_custom_call" | custom-call | tf_op jit(solution)/shard_map/pallas_call | solution.py:489
  16.6 0.7 %copy.12 = f32[3,256,1,128]{3,2,1,0:T(1,128)} copy(f32[3,256,1,128]{3,2,1,0:T(1,128)S(1)} %bitcast.4) | data formatting | bytes 786432
